TPU v7x, 32 devices: a whole 2x2x4 slice. The times are simulated.
32 devices in a mesh: lat: 4 (over y, core), lon: 8 (over z, x).
Axes of the slice: x: 2, y: 2, z: 4, core: 2. Of those that a mesh axis runs over, the one named last changes fastest.
Arguments:
- inputs: bfloat16 [8, 24, 96, 192], P(None, 'lat', 'lon'), may hold values from -6 to 6
- cotangent: bfloat16 [8, 24, 96, 192], P(None, 'lat', 'lon'), may hold values from -6 to 6
- qkv_weight: bfloat16 [192, 576], P(None, 'lon'), may hold values from -0.4375 to 0.4375
- proj_weight: bfloat16 [192, 192], P(None, 'lon'), may hold values from -0.4375 to 0.4375
- up_weight: bfloat16 [192, 768], P(None, 'lon'), may hold values from -0.4375 to 0.4375
- down_weight: bfloat16 [768, 192], P(None, 'lon'), may hold values from -0.21875 to 0.21875
- norm_gains: bfloat16 [2, 192], P(None, 'lon'), may hold values from 0.099609375 to 1.8984375
- bias_table: bfloat16 [16, 6, 20736], P(None, None, 'lon'), may hold values from -4 to 304
- type_of: int32 [4, 4], replicated, may hold values from 0 to 15
- region: int32 [8, 24], P(None, 'lat'), may hold values from 0 to 2
Outputs:
- grad_input: bfloat16 [8, 24, 96, 192], P(None, 'lat', 'lon')
- grad_qkv: float32 [192, 576], P(None, 'lon')
- grad_proj: float32 [192, 192], P(None, 'lon')
- grad_up: float32 [192, 768], P(None, 'lon')
- grad_down: float32 [768, 192], P(None, 'lon')
- grad_gains: float32 [2, 192], P(None, 'lon')
- grad_table: float32 [16, 6, 20736], P(None, None, 'lon')
Inputs may be any that keep to these rules, and one draw needn't show every extreme that they name: `type_of`: types may repeat and some may be absent. Attention joins only tokens of a window with equal region ids.
All inputs are finite; a program needn't handle non-finite values.
Results may differ from a plain program's by a relative error of at most 0.015.
Values may be sent and summed in bfloat16 or wider, within the bound.
A program may use at most 64 MiB of HBM per device.

v0:
```python
import functools
import math

import jax
import jax.numpy as jnp
from jax import lax
from jax.experimental import pallas as pl
from jax.experimental.pallas import tpu as pltpu
from jax.sharding import PartitionSpec as P

WPL = 2
WLAT = 6
WLON = 12
WIN = 144
MESH = pl.DeviceIdType.MESH
F32 = jnp.float32
BF16 = jnp.bfloat16


def layer_norm(values):
    row_mean = jnp.mean(values, axis=-1, keepdims=True)
    centred = values - row_mean
    variance = jnp.mean(centred * centred, axis=-1, keepdims=True)
    inv_std = lax.rsqrt(variance + 1e-05)
    return (centred * inv_std, inv_std)


def norm_back(d_normed, normed, inv_std):
    return inv_std * (
        d_normed
        - jnp.mean(d_normed, axis=-1, keepdims=True)
        - normed * jnp.mean(d_normed * normed, axis=-1, keepdims=True)
    )


def gelu_pair(pre_act):
    cumul = 0.5 * (1.0 + lax.erf(pre_act * 0.7071067811865476))
    density = jnp.exp(-0.5 * pre_act * pre_act) * 0.3989422804014327
    return (pre_act * cumul, cumul + pre_act * density)


def position(nlat, nlon):
    lat, lon = lax.axis_index("lat"), lax.axis_index("lon")

    def at(dlat, dlon):
        return (lax.rem(lat + dlat + nlat, nlat), lax.rem(lon + dlon + nlon, nlon))

    core, side = lax.rem(lat, 2), lax.rem(lon, 2)
    twin = (lat + 1 - 2 * core, lon)
    across = (lat, lon + 1 - 2 * side)
    return lat, lon, at, core, twin, across


def greet(devices):
    barrier = pltpu.get_barrier_semaphore()
    for device in devices:
        pl.semaphore_signal(barrier, inc=1, device_id=device, device_id_type=MESH)
    pl.semaphore_wait(barrier, len(devices))


def peers(nlat, nlon, at, twin, across):
    steps = [(0, d) for d in range(2, nlon, 2)] + [(d, 0) for d in range(2, nlat, 2)]
    steps += [(1, 0), (-1, 0), (0, 1), (0, -1), (1, 1), (-1, -1)]
    return [twin, across] + [at(*step) for step in steps]


def send(src, dst, send_sem, recv_sem, device):
    copy = pltpu.make_async_remote_copy(
        src_ref=src, dst_ref=dst, send_sem=send_sem, recv_sem=recv_sem, device_id=device, device_id_type=MESH
    )
    copy.start()
    return copy


def gather_kernel(nlat, nlon, a, d, b, h_lat, h_lon, h_diag, a_all, d_all, b_all, r_lat, r_lon, r_diag,
                  zs, zr, xs, xr, ts, tr, hs, hr):
    lat, lon, at, core, twin, across = position(nlat, nlon)
    greet(peers(nlat, nlon, at, twin, across))
    reach = nlon // 2
    srcs = (a.at[core], d.at[core], b)

    def slots(owner):
        return (a_all.at[owner, core], d_all.at[owner, core], b_all.at[owner])

    far, near, shared, halo = {}, {}, [], []
    for k in range(1, reach):
        for i in range(3):
            far[i, k] = send(srcs[i], slots(lon)[i], zs.at[i, k], zr.at[i, k], at(0, 2 * k))
    for i in range(3):
        near[i, 0] = send(srcs[i], slots(lon)[i], xs.at[i, 0], xr.at[i, 0], across)
    for i, (src, dst, step) in enumerate(
        ((h_lat, r_lat, (-1, 0)), (h_lon, r_lon, (0, -1)), (h_diag, r_diag, (-1, -1)))
    ):
        halo.append(send(src, dst, hs.at[i], hr.at[i], at(*step)))
    a_all[lon] = a[...]
    d_all[lon] = d[...]
    b_all[lon] = b[...]
    for k in range(1, reach):
        owner = lax.rem(lon - 2 * k + nlon, nlon)
        for i in range(3):
            slot = slots(owner)[i]
            far[i, k].wait_recv()
            near[i, k] = send(slot, slot, xs.at[i, k], xr.at[i, k], across)
            if i < 2:
                shared.append(send(slot, slot, ts.at[i, k], tr.at[i, k], twin))
    for k in range(reach):
        owner = lax.rem(across[1] - 2 * k + nlon, nlon)
        for i in range(3):
            slot = slots(owner)[i]
            near[i, k].wait_recv()
            if i < 2:
                shared.append(send(slot, slot, ts.at[i, reach + k], tr.at[i, reach + k], twin))
    for copy in list(far.values()) + list(near.values()):
        copy.wait_send()
    for copy in halo + shared:
        copy.wait()


def reduce_kernel(nlat, nlon, scale, a, d, t, kron, h_lat, h_lon, h_diag, a_out, d_out, t_out, r_lat, r_lon, r_diag,
                  a_twin, d_twin, a_half, d_half, a_x, d_x, t_x, a_mid, d_mid, t_mid, a_z, d_z, t_z,
                  a_row, d_row, t_row, cs, cr, xs, xr, zs, zr, ls, lr, fs, fr, hs, hr):
    lat, lon, at, core, twin, across = position(nlat, nlon)
    greet(peers(nlat, nlon, at, twin, across))
    reach = nlon // 2
    near, far, rest = {}, {}, []
    order = list(range(1, reach)) + [0]
    pairs = [
        send(src.at[1 - core], dst, cs.at[i], cr.at[i], twin)
        for i, (src, dst) in enumerate(((a, a_twin), (d, d_twin)))
    ]

    def cross(i, src, dst):
        for k in order:
            owner = lax.rem(across[1] + 2 * k, nlon)
            near[i, k] = send(src.at[owner], dst.at[k], xs.at[i, k], xr.at[i, k], across)

    cross(2, t, t_x)
    for i, (src, dst, step) in enumerate(
        ((h_lat, r_lat, (1, 0)), (h_lon, r_lon, (0, 1)), (h_diag, r_diag, (1, 1)))
    ):
        rest.append(send(src, dst, hs.at[i], hr.at[i], at(*step)))
    for i, (own, got, half, dst) in enumerate(((a, a_twin, a_half, a_x), (d, d_twin, d_half, d_x))):
        pairs[i].wait()
        half[...] = (own[core].astype(F32) + got[...].astype(F32)).astype(BF16)
        cross(i, half, dst)
    streams = ((2, t, t_x, t_mid, t_z), (0, a_half, a_x, a_mid, a_z), (1, d_half, d_x, d_mid, d_z))
    for i, own, got, mid, dst in streams:
        for k in range(1, reach):
            owner = lax.rem(lon + 2 * k, nlon)
            near[i, k].wait_recv()
            mid[k] = (own[owner].astype(F32) + got[k].astype(F32)).astype(BF16)
            far[i, k] = send(mid.at[k], dst.at[k], zs.at[i, k], zr.at[i, k], at(0, 2 * k))
    rows = nlat // 2
    row = lax.div(lat, 2)

    def total_of(i, own, got, dst):
        near[i, 0].wait_recv()
        total = own[lon].astype(F32) + got[0].astype(F32)
        for k in range(1, reach):
            far[i, k].wait_recv()
            total = total + dst[k].astype(F32)
        return total.astype(BF16)

    t_row[lat] = total_of(2, t, t_x, t_z)
    rest.append(send(t_row.at[lat], t_row.at[lat], ls.at[2, 0], lr.at[2, 0], twin))
    t_far = [send(t_row.at[lat], t_row.at[lat], ls.at[2, j], lr.at[2, j], at(2 * j, 0)) for j in range(1, rows)]
    halves = []
    for i, own, got, dst, line in ((0, a_half, a_x, a_z, a_row), (1, d_half, d_x, d_z, d_row)):
        line[row] = total_of(i, own, got, dst)
        halves.append(
            [send(line.at[row], line.at[row], ls.at[i, j], lr.at[i, j], at(2 * j, 0)) for j in range(1, rows)]
        )
    for j in range(1, rows):
        slot = t_row.at[lax.rem(lat - 2 * j + nlat, nlat)]
        t_far[j - 1].wait_recv()
        rest.append(send(slot, slot, fs.at[2, j], fr.at[2, j], twin))
    for i, (line, out) in enumerate(((a_row, a_out), (d_row, d_out))):
        for copy in halves[i]:
            copy.wait_recv()
        total = line[0].astype(F32)
        for j in range(1, rows):
            total = total + line[j].astype(F32)
        out[core] = total * scale
        rest.append(send(out.at[core], out.at[core], fs.at[i, 0], fr.at[i, 0], twin))
    for copy in list(near.values()) + list(far.values()) + t_far + halves[0] + halves[1]:
        copy.wait_send()
    for copy in rest:
        copy.wait()
    total = jnp.zeros(t_out.shape, F32)
    for i in range(nlat):
        total = total + jnp.dot(kron[i], t_row[i], preferred_element_type=F32)
    t_out[...] = total


def comm_call(kernel, collective_id, outs, scratch, operands):
    vmem = pl.BlockSpec(memory_space=pltpu.VMEM)
    return pl.pallas_call(
        kernel,
        out_shape=[jax.ShapeDtypeStruct(*o) for o in outs],
        in_specs=[vmem] * len(operands),
        out_specs=[vmem] * len(outs),
        scratch_shapes=scratch,
        compiler_params=pltpu.CompilerParams(
            collective_id=collective_id, has_side_effects=True, vmem_limit_bytes=48 * 2**20
        ),
    )(*operands)


def to_windows(grid):
    p, l, c = grid.shape[:3]
    shaped = grid.reshape(p // WPL, WPL, l // WLAT, WLAT, c // WLON, WLON, grid.shape[-1])
    return shaped.transpose(4, 0, 2, 1, 3, 5, 6).reshape(-1, grid.shape[-1])


def from_windows(flat, p, l, c):
    shaped = flat.reshape(c // WLON, p // WPL, l // WLAT, WPL, WLAT, WLON, flat.shape[-1])
    return shaped.transpose(1, 3, 2, 4, 0, 5, 6).reshape(p, l, c, flat.shape[-1])


def by_t(x, w_t):
    return lax.dot_general(x, w_t, (((1,), (1,)), ((), ())), preferred_element_type=F32)


def outer(x, y):
    return lax.dot_general(x, y, (((0,), (0,)), ((), ())), preferred_element_type=F32)


def plain(x, y):
    return jnp.dot(x, y, preferred_element_type=F32)


def pick_kernel(types, table, out):
    positions = types.shape[0]
    rows = [table[types[i]].astype(F32) for i in range(positions)]
    out[...] = jnp.concatenate(rows, axis=0).astype(BF16)


def pick_rows(types, table):
    _, head_count, part = table.shape
    return pl.pallas_call(
        pick_kernel,
        out_shape=jax.ShapeDtypeStruct((types.shape[0] * head_count, part), BF16),
        in_specs=[pl.BlockSpec(memory_space=pltpu.SMEM), pl.BlockSpec(memory_space=pltpu.VMEM)],
        out_specs=pl.BlockSpec(memory_space=pltpu.VMEM),
    )(types, table)


def window_kernel(n_up, n_qkv, n_proj, cells, cots, a_all, d_all, bias, label_col, label_row,
                  d_cells, ga, gd, table,
                  probs_s, qkv_t, proj_t, up_t, down_t, gains, g_qkv, g_proj, g_up, g_down, g_gain):
    owners, height = a_all.shape[0], a_all.shape[2]

    def joined(half, start, count):
        rows = [a_all[j, half].astype(F32)[start : start + count] for j in range(owners)]
        return jnp.concatenate(rows, axis=0).astype(BF16)

    up_t[...] = joined(0, 0, n_up)
    qkv_t[...] = joined(1, 0, n_qkv)
    proj_t[...] = joined(1, n_qkv, n_proj)
    wide = d_all.shape[3]
    for i in range(2):
        rows = [d_all[j, i].astype(F32) for j in range(owners)]
        down_t[:, i * wide : (i + 1) * wide] = jnp.concatenate(rows, axis=0).astype(BF16)
    gain_sum = a_all[0, 0].astype(F32)[n_up : n_up + 2]
    for j in range(1, owners):
        gain_sum = gain_sum + a_all[j, 0].astype(F32)[n_up : n_up + 2]
    gains[...] = gain_sum
    positions, head_count = bias.shape[:2]
    windows, _, features = cells.shape
    head_size = features // head_count
    factor = 1.0 / math.sqrt(head_size)
    for total in (g_qkv, g_proj, g_up, g_down, g_gain):
        total[...] = jnp.zeros(total.shape, F32)
    if windows > positions:
        table[...] = jnp.zeros(table.shape, F32)

    def body(w, carry):
        p = lax.rem(w, positions)
        gain_one, gain_two = gains[0:1], gains[1:2]
        lane_head = lax.broadcasted_iota(jnp.int32, (1, features), 1) // head_size
        heads = [(lane_head == h).astype(BF16) for h in range(head_count)]
        normed_one, inv_one = layer_norm(cells[w].astype(F32))
        scaled_one = (normed_one * gain_one).astype(BF16)
        q, k, v = (
            by_t(scaled_one, qkv_t[i * features : (i + 1) * features]).astype(BF16) for i in range(3)
        )
        same = label_col[p] == label_row[p]
        attended = jnp.zeros((WIN, features), F32)
        for h, head in enumerate(heads):
            scores = by_t(q * head, k) * factor + bias[p, h].astype(F32)
            scores = jnp.where(same, scores, -jnp.inf)
            raised = jnp.exp(scores - jnp.max(scores, axis=-1, keepdims=True))
            probs = raised * (1.0 / jnp.sum(raised, axis=-1, keepdims=True))
            probs_s[h] = probs
            attended = attended + plain(probs.astype(BF16), v * head)
        attended = attended.astype(BF16)
        middle = cells[w].astype(F32) + by_t(attended, proj_t[...])
        normed_two, inv_two = layer_norm(middle)
        scaled_two = (normed_two * gain_two).astype(BF16)
        cot = cots[w]
        activated, slope = gelu_pair(by_t(scaled_two, up_t[...]))
        g_down[...] += outer(cot, activated.astype(BF16))
        d_hidden = (plain(cot, down_t[...]) * slope).astype(BF16)
        g_up[...] += outer(d_hidden, scaled_two)
        d_htwo = plain(d_hidden, up_t[...])
        g_gain[1:2] += jnp.sum(d_htwo * normed_two, axis=0, keepdims=True)
        d_middle = cot.astype(F32) + norm_back(d_htwo * gain_two, normed_two, inv_two)
        d_middle_b = d_middle.astype(BF16)
        g_proj[...] += outer(d_middle_b, attended)
        d_att = plain(d_middle_b, proj_t[...]).astype(BF16)
        d_q, d_k, d_v = (jnp.zeros((WIN, features), F32) for _ in range(3))
        for h, head in enumerate(heads):
            probs, d_att_h = probs_s[h], d_att * head
            d_prob = by_t(d_att_h, v)
            d_v = d_v + outer(probs.astype(BF16), d_att_h)
            d_score = probs * (d_prob - jnp.sum(probs * d_prob, axis=-1, keepdims=True))
            if windows > positions:
                table[p, h] += d_score
            else:
                table[p, h] = d_score.astype(table.dtype)
            d_score_b = d_score.astype(BF16)
            d_q = d_q + plain(d_score_b, k * head)
            d_k = d_k + outer(d_score_b, q * head)
        d_hone = jnp.zeros((WIN, features), F32)
        for i, part in enumerate((d_q * factor, d_k * factor, d_v)):
            part = part.astype(BF16)
            span = slice(i * features, (i + 1) * features)
            g_qkv[span] += outer(part, scaled_one)
            d_hone = d_hone + plain(part, qkv_t[span])
        g_gain[0:1] += jnp.sum(d_hone * normed_one, axis=0, keepdims=True)
        d_cells[w] = (d_middle + norm_back(d_hone * gain_one, normed_one, inv_one)).astype(BF16)
        return carry

    lax.fori_loop(0, windows, body, 0)
    features = cells.shape[2]
    down = d_all.shape[2]
    gain_rows = jnp.concatenate([g_gain[...], jnp.zeros((height - n_up - 2, features), F32)], axis=0)
    spare = height - n_qkv - n_proj
    for j in range(owners):
        ga[0, j] = jnp.concatenate([g_up[j * n_up : (j + 1) * n_up], gain_rows], axis=0).astype(BF16)
        rows = [g_qkv[j * n_qkv : (j + 1) * n_qkv], g_proj[j * n_proj : (j + 1) * n_proj]]
        rows += [jnp.zeros((spare, features), F32)] if spare else []
        ga[1, j] = jnp.concatenate(rows, axis=0).astype(BF16)
        for i in range(2):
            gd[i, j] = g_down[j * down : (j + 1) * down, i * wide : (i + 1) * wide].astype(BF16)


def block_grads(cells, cots, a_all, d_all, cuts, bias, labels):
    features = cells.shape[1]
    positions, head_count = bias.shape[:2]
    windows, owners, wide = cells.shape[0] // WIN, a_all.shape[0], d_all.shape[3] * 2
    vmem = pl.BlockSpec(memory_space=pltpu.VMEM)
    outs = [((windows, WIN, features), BF16)]
    outs += [((2, owners) + x.shape[2:], BF16) for x in (a_all, d_all)]
    outs += [(bias.shape, F32 if windows > positions else BF16)]
    n_up, n_qkv, n_proj = cuts
    sizes = [(owners * n, features) for n in (n_qkv, n_proj, n_up)] + [(features, wide)]
    d_cells, *grads = pl.pallas_call(
        functools.partial(window_kernel, *cuts),
        out_shape=[jax.ShapeDtypeStruct(*o) for o in outs],
        in_specs=[vmem] * 7,
        out_specs=[vmem] * len(outs),
        scratch_shapes=[pltpu.VMEM((head_count, WIN, WIN), F32)]
        + [pltpu.VMEM(size, BF16) for size in sizes] + [pltpu.VMEM((2, features), F32)]
        + [pltpu.VMEM(size, F32) for size in sizes] + [pltpu.VMEM((2, features), F32)],
        compiler_params=pltpu.CompilerParams(vmem_limit_bytes=48 * 2**20),
    )(
        cells.reshape(windows, WIN, features), cots.reshape(windows, WIN, features),
        a_all, d_all, bias, labels[:, :, None], labels[:, None, :],
    )
    return (d_cells.reshape(cells.shape), *grads)


def shards(inputs, cotangent, qkv_weight, proj_weight, up_weight, down_weight, norm_gains, bias_table, type_of, region):
    levels, rows, cols, features = inputs.shape
    nlat, nlon = lax.axis_size("lat"), lax.axis_size("lon")
    level_windows, row_windows = levels // WPL, rows // WLAT
    type_count, head_count, part = bias_table.shape
    positions = level_windows * row_windows
    lat_index = lax.axis_index("lat")
    row_half, col_half, level_shift = WLAT // 2, WLON // 2, WPL // 2
    all_types = type_of.reshape(level_windows, nlat, row_windows).transpose(1, 0, 2).reshape(nlat, positions)
    types = lax.dynamic_index_in_dim(all_types, lat_index, 0, keepdims=False)
    n_up, n_qkv, n_proj = up_weight.shape[1], qkv_weight.shape[1], proj_weight.shape[1]
    gain_cols, height = norm_gains.shape[1], -(-max(n_up + 2, n_qkv + n_proj) // 8) * 8
    gain_spot = lax.axis_index("lon") * gain_cols
    own_lane = jnp.arange(features, dtype=jnp.int32) // gain_cols == lax.axis_index("lon")
    gain_rows = jnp.where(own_lane, jnp.tile(norm_gains, (1, nlon)), jnp.zeros((), BF16))
    gain_rows = jnp.pad(gain_rows, ((0, height - n_up - 2), (0, 0)))
    a_part = jnp.stack(
        [
            jnp.concatenate([up_weight.T, gain_rows]),
            jnp.pad(
                jnp.concatenate([qkv_weight.T, proj_weight.T]), ((0, height - n_qkv - n_proj), (0, 0))
            ),
        ]
    )
    d_part = down_weight.reshape(2, -1, down_weight.shape[1]).transpose(0, 2, 1)
    b_part = pick_rows(types, bias_table)
    both = jnp.roll(jnp.stack([inputs, cotangent]), -level_shift, axis=1)
    rim_lat = both[:, :, :row_half, col_half:]
    rim_lon = both[:, :, row_half:, :col_half]
    rim_diag = both[:, :, :row_half, :col_half]
    flat = [r.reshape(-1, features) for r in (rim_lat, rim_lon, rim_diag)]
    dma = pltpu.SemaphoreType.DMA
    a_all, d_all, b_all, r_lat, r_lon, r_diag = comm_call(
        functools.partial(gather_kernel, nlat, nlon),
        0,
        [((nlon,) + x.shape, BF16) for x in (a_part, d_part, b_part)] + [(x.shape, BF16) for x in flat],
        [dma((3, nlon // 2))] * 4 + [dma((2, nlon))] * 2 + [dma((3,))] * 2,
        (a_part, d_part, b_part, *flat),
    )
    bias = b_all.transpose(1, 0, 2).reshape(positions, head_count, WIN, WIN)
    top = jnp.concatenate([both[:, :, row_half:, col_half:], r_lon.reshape(rim_lon.shape)], axis=3)
    bottom = jnp.concatenate([r_lat.reshape(rim_lat.shape), r_diag.reshape(rim_diag.shape)], axis=3)
    shifted = jnp.concatenate([top, bottom], axis=2)
    labels = region.reshape(level_windows, WPL, row_windows, WLAT).transpose(0, 2, 1, 3)
    labels = jnp.broadcast_to(labels[..., None], labels.shape + (WLON,)).reshape(positions, WIN)
    d_cells, ga, gd, table = block_grads(
        to_windows(shifted[0]), to_windows(shifted[1]), a_all, d_all, (n_up, n_qkv, n_proj), bias, labels
    )
    gt = table.astype(BF16).reshape(positions * head_count, nlon, part).transpose(1, 0, 2)
    onehot = (all_types[:, None, :] == jnp.arange(type_count, dtype=jnp.int32)[None, :, None]).astype(BF16)
    kron = jnp.einsum("lyp,gh->lygph", onehot, jnp.eye(head_count, dtype=BF16)).reshape(
        nlat, type_count * head_count, positions * head_count
    )
    back = from_windows(d_cells, levels, rows, cols)
    out_lat = back[:, rows - row_half :, : cols - col_half]
    out_lon = back[:, : rows - row_half, cols - col_half :]
    out_diag = back[:, rows - row_half :, cols - col_half :]
    flat = [r.reshape(-1, features) for r in (out_lat, out_lon, out_diag)]
    shard_shapes = (ga.shape[2:], gd.shape[2:], gt.shape[1:])
    token_count = levels * rows * cols * nlat * nlon
    a_sum, d_sum, t_sum, r_lat, r_lon, r_diag = comm_call(
        functools.partial(reduce_kernel, nlat, nlon, 1.0 / math.sqrt(token_count)),
        1,
        [((2,) + ga.shape[2:], F32), ((2,) + gd.shape[2:], F32), ((type_count * head_count, part), F32)]
        + [(x.shape, BF16) for x in flat],
        [pltpu.VMEM(x.shape[1:], BF16) for x in (ga, gd)] * 2
        + [pltpu.VMEM((nlon // 2,) + shape, BF16) for shape in shard_shapes] * 3
        + [pltpu.VMEM((nlat // 2,) + shape, BF16) for shape in shard_shapes[:2]]
        + [pltpu.VMEM((nlat,) + shard_shapes[2], BF16)]
        + [dma((2,))] * 2 + [dma((3, nlon // 2))] * 4 + [dma((3, nlat // 2))] * 4 + [dma((3,))] * 2,
        (ga, gd, gt, kron, *flat),
    )
    own = back[:, : rows - row_half, : cols - col_half]
    top = jnp.concatenate([r_diag.reshape(out_diag.shape), r_lat.reshape(out_lat.shape)], axis=2)
    bottom = jnp.concatenate([r_lon.reshape(out_lon.shape), own], axis=2)
    grad_input = jnp.roll(jnp.concatenate([top, bottom], axis=1), level_shift, axis=0)
    return (
        grad_input,
        a_sum[1, :n_qkv].T,
        a_sum[1, n_qkv : n_qkv + n_proj].T,
        a_sum[0, :n_up].T,
        d_sum.transpose(0, 2, 1).reshape(down_weight.shape),
        lax.dynamic_slice(a_sum[0, n_up : n_up + 2], (jnp.int32(0), gain_spot), (2, gain_cols)),
        t_sum.reshape(type_count, head_count, part),
    )


def solution(mesh):
    return jax.shard_map(
        shards,
        mesh=mesh,
        in_specs=(
            P(None, "lat", "lon", None),
            P(None, "lat", "lon", None),
            P(None, "lon"),
            P(None, "lon"),
            P(None, "lon"),
            P(None, "lon"),
            P(None, "lon"),
            P(None, None, "lon"),
            P(),
            P(None, "lat"),
        ),
        out_specs=(
            P(None, "lat", "lon", None),
            P(None, "lon"),
            P(None, "lon"),
            P(None, "lon"),
            P(None, "lon"),
            P(None, "lon"),
            P(None, None, "lon"),
        ),
        check_vma=False,
    )
```

profile of v0, /device:TPU:0, one launch (start us, length us, event | category | flops | bytes accessed | tf_op | source)
XLA Modules:
  0.0 124.7 jit_solution(17269702392092154490)
XLA Ops:
  0.6 1.2 copy_bitcast_fusion.1
  2.9 0.7 dynamic-slice_reduce_fusion.types
  3.5 1.0 copy.39.table
  4.5 1.8 %shard_map.153.b = bf16[24,2592]{1,0:T(8,128)(2,1)} custom-call(s32[4]{0:T(128)} %dynamic-slice_reduce_fusion.types, bf16[16,6,2592]{2,1,0:T(8,128)(2,1)} %copy.39.table), custom_call_target="tpu_custom_call" | custom-call | tf_op jit(solution)/shard_map/pallas_call | solution.py:240
  6.7 0.9 copy-done.2
  7.6 32.6 %shard_map.154 = (bf16[8,2,104,192]{3,2,1,0:T(8,128)(2,1)S(1)}, bf16[8,2,24,384]{3,2,1,0:T(8,128)(2,1)S(1)}, bf16[8,24,2592]{2,1,0:T(8,128)(2,1)S(1)}, bf16[288,...) custom-call(bf16[2,104,192]{2,1,0:T(8,128)(2,1)S(1)} %pad_maximum_fusion.5.a, ...), custom_call_target="tpu_custom_call" | custom-call | tf_op jit(solution)/shard_map/pallas_call | solution.py:197
  40.2 0.9 copy-done
  41.1 0.7 copy-done.5
  42.8 2.3 %reshape.100.bias = bf16[4,6,144,144]{3,2,1,0:T(8,128)(2,1)} reshape(bf16[24,8,2592]{2,1,0:T(8,128)(2,1)S(1)} %copy.40) | data formatting | bytes 1990656 | tf_op jit(solution)/shard_map/reshape | solution.py:413
  45.4 1.1 copy-done.1
  46.5 1.0 copy-done.6
  47.5 19.2 %shard_map.155 = (bf16[4,144,192]{2,1,0:T(8,128)(2,1)S(1)}, bf16[2,8,104,192]{3,2,1,0:T(8,128)(2,1)S(1)}, bf16[2,8,24,384]{3,2,1,0:T(8,128)(2,1)S(1)}, bf16[4,6,144,144]{3,2,1,0:T(8,128)(2,1)S(1)}) custom-call(bf16[4,144,192]{2,1,0:T(8,128)(2,1)S(1)} %reshape_reshape_transpose_reshape_squeeze.6.cells, ...), custom_call_target="tpu_custom_call" | custom-call | tf_op jit(solution)/shard_map/pallas_call | solution.py:358
  66.7 0.7 copy-done.3
  67.4 0.7 copy-done.8
  68.1 2.2 %reshape.101 = bf16[24,8,2592]{2,1,0:T(8,128)(2,1)} reshape(bf16[4,6,144,144]{3,2,1,0:T(8,128)(2,1)S(1)} %get-tuple-element.31) | data formatting | bytes 1990656 | tf_op jit(solution)/shard_map/reshape | solution.py:422
  70.4 1.4 %copy.56 = bf16[24,8,2592]{2,0,1:T(8,128)(2,1)S(1)} copy(bf16[24,8,2592]{2,1,0:T(8,128)(2,1)} %reshape.101) | data formatting | bytes 1990656 | tf_op jit(solution)/shard_map/reshape | solution.py:422
  71.8 0.7 fusion.17
  72.7 0.7 reshape.106.h_diag
  74.1 0.9 copy-done.7
  75.0 40.6 %shard_map.156 = (f32[2,104,192]{2,1,0:T(8,128)S(1)}, f32[2,24,384]{2,1,0:T(8,128)S(1)}, f32[96,2592]{1,0:T(8,128)S(1)}, bf16[144,192]{1,0:T(8,128)(2,1)S(1)}, b...) custom-call(bf16[2,8,104,192]{3,2,1,0:T(8,128)(2,1)S(1)} %get-tuple-element.29.a, ...), custom_call_target="tpu_custom_call" | custom-call | tf_op jit(solution)/shard_map/pallas_call | solution.py:197
  115.7 0.7 copy-done.10
  119.1 1.1 copy.49
  120.5 0.9 copy.47
  121.4 0.7 copy.48
  (94 shorter events, 8.9 us)
Async XLA Ops:
  2.2 0.7 copy-start.26
  2.2 1.4 %copy-start.20 = (bf16[16,6,2592]{2,0,1:T(8,128)(2,1)S(1)}, bf16[16,6,2592]{2,0,1:T(8,128)(2,1)}, u32[]{:S(2)}) copy-start(bf16[16,6,2592]{2,0,1:T(8,128)(2,1)} %param.17) | copy-start | bytes 1492996
  2.3 4.0 %copy-start.28 = (bf16[2,24]{1,0:T(2,128)(2,1)S(1)}, bf16[2,24]{1,0:T(2,128)(2,1)}, u32[]{:S(2)}) copy-start(bf16[2,24]{1,0:T(2,128)(2,1)} %param.16) | copy-start | bytes 292
  2.3 4.1 %copy-start.22 = (bf16[192,96]{1,0:T(8,128)(2,1)S(1)}, bf16[192,96]{1,0:T(8,128)(2,1)}, u32[]{:S(2)}) copy-start(bf16[192,96]{1,0:T(8,128)(2,1)} %param.14) | copy-start | bytes 110596
  2.4 4.2 %copy-start.23 = (bf16[192,72]{0,1:T(8,128)(2,1)S(1)}, bf16[192,72]{0,1:T(8,128)(2,1)}, u32[]{:S(2)}) copy-start(bf16[192,72]{0,1:T(8,128)(2,1)} %param.12) | copy-start | bytes 82948
  2.4 4.2 %copy-start.25 = (bf16[192,24]{0,1:T(8,128)(2,1)S(1)}, bf16[192,24]{0,1:T(8,128)(2,1)}, u32[]{:S(2)}) copy-start(bf16[192,24]{0,1:T(8,128)(2,1)} %param.13) | copy-start | bytes 27652
  2.5 4.2 %copy-start.24 = (bf16[768,24]{0,1:T(8,128)(2,1)S(1)}, bf16[768,24]{0,1:T(8,128)(2,1)}, u32[]{:S(2)}) copy-start(bf16[768,24]{0,1:T(8,128)(2,1)} %param.15) | copy-start | bytes 110596
  6.7 0.9 copy-start.2
  40.2 0.9 copy-start
  41.1 0.7 copy-start.5
  42.8 2.3 %copy-start.27 = (s32[8,6]{1,0:T(8,128)S(1)}, s32[8,6]{1,0:T(8,128)}, u32[]{:S(2)}) copy-start(s32[8,6]{1,0:T(8,128)} %param.19) | copy-start | bytes 580
  45.3 1.2 copy-start.1
  46.5 1.0 copy-start.6
  66.7 0.7 copy-start.3
  67.4 0.7 copy-start.8
  70.4 1.4 %copy-start.9 = (bf16[4,144,192]{2,1,0:T(8,128)(2,1)S(1)}, bf16[4,144,192]{2,1,0:T(8,128)(2,1)}, u32[]{:S(2)}) copy-start(bf16[4,144,192]{2,1,0:T(8,128)(2,1)} %copy-done.8) | copy-start | bytes 663556
  71.7 2.4 %copy-start.4 = (bf16[2,8,24,384]{3,2,1,0:T(8,128)(2,1)S(1)}, bf16[2,8,24,384]{3,2,1,0:T(8,128)(2,1)}, u32[]{:S(2)}) copy-start(bf16[2,8,24,384]{3,2,1,0:T(8,128)(2,1)} %copy-done.3) | copy-start | bytes 884740
  74.1 0.9 copy-start.7
  119.0 1.2 copy-start.19
  119.0 1.2 copy-start.17
  119.0 1.3 %copy-start.15 = (bf16[144,192]{1,0:T(8,128)(2,1)S(1)}, bf16[144,192]{1,0:T(8,128)(2,1)}, u32[]{:S(2)}) copy-start(bf16[144,192]{1,0:T(8,128)(2,1)} %copy-done.14) | copy-start | bytes 165892
  119.0 1.3 %copy-start.21 = (bf16[8,3,6,192]{3,2,1,0:T(8,128)(2,1)S(1)}, bf16[8,3,6,192]{3,2,1,0:T(8,128)(2,1)}, u32[]{:S(2)}) copy-start(bf16[8,3,6,192]{3,2,1,0:T(8,128)(2,1)} %get-tuple-element.60) | copy-start | bytes 165892
  120.2 1.2 copy-start.11
  120.2 1.9 %copy-start.13 = (f32[2,24,384]{2,1,0:T(8,128)S(1)}, f32[2,24,384]{2,1,0:T(8,128)}, u32[]{:S(2)}) copy-start(f32[2,24,384]{2,1,0:T(8,128)} %copy-done.12) | copy-start | bytes 221188
  (5 other events, 3.2 us)
where the time goes:
time: 125 us
  Pallas kernels  94.2 us (75%)
  local copies, waits for them, and re-layouts  28.3 us (23%)
    pallas_call x2, Pallas kernels, comm_call(): pl.pallas_call(kernel, out_shape=[jax.ShapeDtypeStruct(*o) for o in outs]...  73.2 us
    pallas_call x1, Pallas kernels, block_grads(): pl.pallas_call(functools.partial(window_kernel, *cuts), out_shape=[jax.Sh...  19.2 us
    unnamed x63, local copies, waits for them, and re-layouts  14.2 us
    reshape x2, local copies, waits for them, and re-layouts, shards(): table.astype(BF16).reshape(positions * head_count, nlon, part)  3.6 us

commit v1 on v0

--- a/solution.py
+++ b/solution.py
@@ -371,7 +371,7 @@
     return (d_cells.reshape(cells.shape), *grads)
 
 
-def shards(inputs, cotangent, qkv_weight, proj_weight, up_weight, down_weight, norm_gains, bias_table, type_of, region):
+def shards_plain(inputs, cotangent, qkv_weight, proj_weight, up_weight, down_weight, norm_gains, bias_table, type_of, region):
     levels, rows, cols, features = inputs.shape
     nlat, nlon = lax.axis_size("lat"), lax.axis_size("lon")
     level_windows, row_windows = levels // WPL, rows // WLAT
@@ -456,6 +456,626 @@
         lax.dynamic_slice(a_sum[0, n_up : n_up + 2], (jnp.int32(0), gain_spot), (2, gain_cols)),
         t_sum.reshape(type_count, head_count, part),
     )
+
+
+LANES = 128
+SUB = 8
+
+
+def rc(src, dst, send_sem, recv_sem, device):
+    return pltpu.make_async_remote_copy(
+        src_ref=src, dst_ref=dst, send_sem=send_sem, recv_sem=recv_sem, device_id=device, device_id_type=MESH
+    )
+
+
+def fused_kernel(nlat, nlon, cuts, scale, x_in, c_in, a, d, tab, types, label_q, label_k,
+                 out, qkv_o, proj_o, up_o, down_o, gain_o, t_out,
+                 grid, a_all, d_all, b_all,
+                 wide_s, cells_s, cots_s, dcell_s, perm_s, asm_s, score_s, prob_b, ds_b, kexp_s, vexp_s,
+                 pick_m, pick_t, pick_u,
+                 qkv_t, proj_t, up_t, down_t, gains, g_qkv, g_proj, g_up, g_down, g_gain,
+                 ga, gd, obuf, a_twin, d_twin, a_half, d_half, a_x, d_x, a_mid, d_mid, a_z, d_z, a_row, d_row,
+                 a_fin, d_fin, t_w, t_x, t_mid, t_z, t_row, t_val,
+                 own_s, hs, hr, wzs, wzr, wxs, wxr, wts, wtr, bzs, bzr, bxs, bxr,
+                 txs, txr, tzs, tzr, tls, tlr, tfs, tfr,
+                 pcs, pcr, pxs, pxr, pzs, pzr, pls, plr, pfs, pfr, ohs, ohr):
+    n_up, n_qkv, n_proj = cuts
+    lat, lon, at, core, twin, across = position(nlat, nlon)
+    rows_c, cols_c, levels, features = x_in.shape
+    half_r, half_c = rows_c // 2, cols_c // 2
+    head_count = tab.shape[0]
+    type_count = tab.shape[1]
+    positions = label_q.shape[0]
+    owners, height, wide = nlon, a.shape[1], d.shape[2]
+    reach, rows_n = nlon // 2, nlat // 2
+    head_size = features // head_count
+    per = WIN // owners
+    spare = WIN - LANES
+    factor = 1.0 / math.sqrt(head_size)
+    slab = WIN // WPL
+
+    greet(peers(nlat, nlon, at, twin, across))
+
+    tiles = [(t, t * LANES, min(LANES, features - t * LANES)) for t in range(-(-features // LANES))]
+
+    def fill(ref, value):
+        for t, start, count in tiles:
+            ref[t, :, :count] = value[:, start : start + count]
+
+    def whole(ref):
+        return jnp.concatenate([ref[t][:, :count] for t, _, count in tiles], axis=1)
+
+    def strided(ref, start, size, stride):
+        return jnp.concatenate(
+            [ref.at[t][pl.ds(start, size, stride=stride), :][:, :count] for t, _, count in tiles], axis=1
+        )
+
+    def store_strided(ref, start, size, stride, value):
+        for t, first, count in tiles:
+            piece = value[:, first : first + count]
+            if count < LANES:
+                piece = jnp.concatenate([piece, jnp.zeros((size, LANES - count), F32)], axis=1)
+            ref.at[t][pl.ds(start, size, stride=stride), :] = piece
+
+    def w_slots(owner):
+        return (a_all.at[owner, core], d_all.at[owner, core])
+
+    w_src = (a.at[core], d.at[core])
+
+    def far_w(i, k):
+        return rc(w_src[i], w_slots(lon)[i], wzs.at[i, k], wzr.at[i, k], at(0, 2 * k))
+
+    for i in (0, 1):
+        for k in range(1, reach):
+            far_w(i, k).start()
+        rc(w_src[i], w_slots(lon)[i], wxs.at[i, 0], wxr.at[i, 0], across).start()
+    lo_r, hi_r = pl.ds(0, half_r), pl.ds(half_r, rows_c - half_r)
+    lo_c, hi_c = pl.ds(0, half_c), pl.ds(half_c, cols_c - half_c)
+    end_r, end_c = pl.ds(rows_c - half_r, half_r), pl.ds(cols_c - half_c, half_c)
+    first_r, first_c = pl.ds(0, rows_c - half_r), pl.ds(0, cols_c - half_c)
+
+    def halo(g, i):
+        src = (x_in, c_in)[g]
+        dst = grid.at[g]
+        if i == 0:
+            return rc(src.at[lo_r, hi_c], dst.at[end_r, first_c], hs.at[g, i], hr.at[g, i], at(-1, 0))
+        if i == 1:
+            return rc(src.at[hi_r, lo_c], dst.at[first_r, end_c], hs.at[g, i], hr.at[g, i], at(0, -1))
+        return rc(src.at[lo_r, lo_c], dst.at[end_r, end_c], hs.at[g, i], hr.at[g, i], at(-1, -1))
+
+    def own(g):
+        return pltpu.make_async_copy((x_in, c_in)[g].at[hi_r, hi_c], grid.at[g].at[first_r, first_c], own_s.at[g])
+
+    for g in (0, 1):
+        own(g).start()
+        for i in range(3):
+            halo(g, i).start()
+
+    rows_i = lax.broadcasted_iota(jnp.int32, (SUB, type_count), 0)
+    want = jnp.full((SUB, type_count), -1, jnp.int32)
+    for i in range(positions):
+        want = jnp.where(rows_i == i, types[i, lat], want)
+    onehot = (lax.broadcasted_iota(jnp.int32, (SUB, type_count), 1) == want).astype(F32).astype(BF16)
+    tails = [jnp.zeros((per, LANES), F32) for _ in range(positions)]
+    for h in range(head_count):
+        val = jnp.dot(onehot, tab[h], preferred_element_type=F32)
+        for r in range(per):
+            pick_m[r * SUB : (r + 1) * SUB] = val[:, r * WIN : r * WIN + LANES]
+            end = val[:, r * WIN + LANES : (r + 1) * WIN]
+            pick_t[r * SUB : (r + 1) * SUB] = jnp.concatenate([end, jnp.zeros((SUB, LANES - spare), F32)], axis=1)
+        for i in range(positions):
+            pick_u[i, pl.ds(h, per, stride=SUB), :] = pick_m[pl.ds(i, per, stride=SUB), :]
+            piece = pick_t[pl.ds(i, per, stride=SUB), :]
+            tails[i] = tails[i] + (pltpu.roll(piece, h * spare, 1) if h else piece)
+    for i in range(positions):
+        pick_u[i, pl.ds(head_count, per, stride=SUB), :] = tails[i]
+        for h in range(head_count + 1, SUB):
+            pick_u[i, pl.ds(h, per, stride=SUB), :] = jnp.zeros((per, LANES), F32)
+
+    def far_b(p, k):
+        return rc(b_all.at[p, lon], b_all.at[p, lon], bzs.at[p, k], bzr.at[p, k], at(0, 2 * k))
+
+    def relay_b(p):
+        rc(b_all.at[p, lon], b_all.at[p, lon], bxs.at[p, 0], bxr.at[p, 0], across).start()
+        for k in range(1, reach):
+            far_b(p, k).wait_recv()
+            slot = b_all.at[p, lax.rem(lon - 2 * k + nlon, nlon)]
+            rc(slot, slot, bxs.at[p, k], bxr.at[p, k], across).start()
+
+    def near_b(p, k):
+        slot = b_all.at[p, lon]
+        return rc(slot, slot, bxs.at[p, k], bxr.at[p, k], across)
+
+    for i in range(positions):
+        b_all[i, lon] = pick_u[i].astype(BF16)
+    for i in range(positions):
+        for k in range(1, reach):
+            far_b(i, k).start()
+
+    a_all[lon] = a[...]
+    d_all[lon] = d[...]
+    shared = []
+    for k in range(1, reach):
+        owner = lax.rem(lon - 2 * k + nlon, nlon)
+        for i in (0, 1):
+            slot = w_slots(owner)[i]
+            far_w(i, k).wait_recv()
+            rc(slot, slot, wxs.at[i, k], wxr.at[i, k], across).start()
+            copy = rc(slot, slot, wts.at[i, k], wtr.at[i, k], twin)
+            copy.start()
+            shared.append(copy)
+    relay_b(0)
+    for g, store in ((0, cells_s), (1, cots_s)):
+        own(g).wait()
+        for i in range(3):
+            halo(g, i).wait_recv()
+        fill(wide_s, grid[g].astype(F32).reshape(rows_c * cols_c * levels, features))
+        for i in range(positions):
+            for j in range(WPL):
+                level = (WPL * i + j + WPL // 2) % levels
+                store[i, j * slab : (j + 1) * slab] = strided(wide_s, level, slab, levels)
+    for k in range(reach):
+        owner = lax.rem(across[1] - 2 * k + nlon, nlon)
+        for i in (0, 1):
+            slot = w_slots(owner)[i]
+            rc(slot, slot, wxs.at[i, k], wxr.at[i, k], across).wait_recv()
+            copy = rc(slot, slot, wts.at[i, reach + k], wtr.at[i, reach + k], twin)
+            copy.start()
+            shared.append(copy)
+    for total in (g_qkv, g_proj, g_up, g_down, g_gain):
+        total[...] = jnp.zeros(total.shape, F32)
+    asm_s[...] = jnp.zeros(asm_s.shape, F32)
+    for copy in shared:
+        copy.wait_recv()
+
+    def joined(half, start, count):
+        rows = [a_all[j, half].astype(F32)[start : start + count] for j in range(owners)]
+        return jnp.concatenate(rows, axis=0).astype(BF16)
+
+    up_t[...] = joined(0, 0, n_up)
+    qkv_t[...] = joined(1, 0, n_qkv)
+    proj_t[...] = joined(1, n_qkv, n_proj)
+    for i in range(2):
+        rows = [d_all[j, i].astype(F32) for j in range(owners)]
+        down_t[:, i * wide : (i + 1) * wide] = jnp.concatenate(rows, axis=0).astype(BF16)
+    gain_sum = a_all[0, 0].astype(F32)[n_up : n_up + 2]
+    for j in range(1, owners):
+        gain_sum = gain_sum + a_all[j, 0].astype(F32)[n_up : n_up + 2]
+    gains[...] = gain_sum
+
+    def near_t(p, k):
+        owner = lax.rem(across[1] + 2 * k, nlon)
+        return rc(t_w.at[p, owner], t_x.at[p, k], txs.at[p, k], txr.at[p, k], across)
+
+    def far_t(p, k):
+        return rc(t_mid.at[p, k], t_z.at[p, k], tzs.at[p, k], tzr.at[p, k], at(0, 2 * k))
+
+    order = list(range(1, reach)) + [0]
+
+    def stage_one(p):
+        for k in order:
+            near_t(p, k).start()
+
+    def stage_two(p):
+        for k in range(1, reach):
+            owner = lax.rem(lon + 2 * k, nlon)
+            near_t(p, k).wait_recv()
+            t_mid[p, k] = (t_w[p, owner].astype(F32) + t_x[p, k].astype(F32)).astype(BF16)
+            far_t(p, k).start()
+
+    def row_t(p, j):
+        slot = t_row.at[lat, p]
+        return rc(slot, slot, tls.at[p, j], tlr.at[p, j], at(2 * j, 0) if j else twin)
+
+    def stage_three(p):
+        near_t(p, 0).wait_recv()
+        total = t_w[p, lon].astype(F32) + t_x[p, 0].astype(F32)
+        for k in range(1, reach):
+            far_t(p, k).wait_recv()
+            total = total + t_z[p, k].astype(F32)
+        t_row[lat, p] = total.astype(BF16)
+        for j in list(range(1, rows_n)) + [0]:
+            row_t(p, j).start()
+
+    def fold_t(p, j):
+        slot = t_row.at[lax.rem(lat - 2 * j + nlat, nlat), p]
+        return rc(slot, slot, tfs.at[p, j], tfr.at[p, j], twin)
+
+    def stage_four(p):
+        for j in range(1, rows_n):
+            row_t(p, j).wait_recv()
+            fold_t(p, j).start()
+
+    lane_head = lax.broadcasted_iota(jnp.int32, (1, features), 1) // head_size
+    seg = lax.broadcasted_iota(jnp.int32, (1, LANES), 1) // spare
+
+    def to_perm(value):
+        fill(perm_s, value)
+        return jnp.concatenate([strided(perm_s, r, SUB, per) for r in range(per)], axis=0)
+
+    def from_perm(value):
+        for r in range(per):
+            store_strided(perm_s, r, SUB, per, value[r * SUB : (r + 1) * SUB])
+        return whole(perm_s)
+
+    def expand(dst, rows):
+        low = rows[:LANES]
+        high = rows[LANES:]
+        ends = []
+        for h in range(head_count):
+            mine = lane_head == h
+            dst[h * LANES : (h + 1) * LANES] = jnp.where(mine, low, 0.0).astype(BF16)
+            ends.append(jnp.where(mine, high, 0.0))
+        ends.append(jnp.zeros((LANES - head_count * spare, features), F32))
+        dst[head_count * LANES :] = jnp.concatenate(ends, axis=0).astype(BF16)
+
+    def collapse(big):
+        low = big[:LANES]
+        start = head_count * LANES
+        high = big[start : start + spare]
+        for h in range(1, head_count):
+            mine = lane_head == h
+            low = jnp.where(mine, big[h * LANES : (h + 1) * LANES], low)
+            high = jnp.where(mine, big[start + h * spare : start + (h + 1) * spare], high)
+        return jnp.concatenate([low, high], axis=0)
+
+    def block(h):
+        return slice(h * LANES, (h + 1) * LANES)
+
+    def body(p, carry):
+        gain_one, gain_two = gains[0:1], gains[1:2]
+        normed_one, inv_one = layer_norm(cells_s[p])
+        scaled_one = (normed_one * gain_one).astype(BF16)
+        q, k, v = (by_t(scaled_one, qkv_t[i * features : (i + 1) * features]) for i in range(3))
+        qp = to_perm(q).astype(BF16)
+        expand(kexp_s, k)
+        expand(vexp_s, v)
+        for j in range(reach):
+            near_b(p, j).wait_recv()
+        for j in range(owners):
+            asm_s[j * WIN : (j + 1) * WIN] = b_all[p, j].astype(F32)
+        same = label_q[p] == label_k[p, 0:1]
+        same_end = label_q[p] == label_k[p, 1:2]
+
+        def bias_of(h):
+            return jnp.concatenate([asm_s[pl.ds(r * SUB + h, SUB, stride=WIN), :] for r in range(per)], axis=0)
+
+        def raw(h, keep):
+            scores = by_t(qp, kexp_s[block(h)]) * factor + bias_of(h)
+            return jnp.where(keep, scores, -jnp.inf)
+
+        last = head_count
+        s_end = raw(last, same_end)
+        peak_end = jnp.zeros((WIN, LANES), F32)
+        for h in range(head_count):
+            mine = seg == h
+            s = raw(h, same)
+            peak = jnp.max(jnp.maximum(s, jnp.where(mine, s_end, -jnp.inf)), axis=-1, keepdims=True)
+            score_s[h] = jnp.exp(s - peak)
+            peak_end = jnp.where(mine, peak, peak_end)
+        e_end = jnp.exp(s_end - peak_end)
+        inv_end = jnp.zeros((WIN, LANES), F32)
+        for h in range(head_count):
+            mine = seg == h
+            e = score_s[h]
+            inv = 1.0 / jnp.sum(e + jnp.where(mine, e_end, 0.0), axis=-1, keepdims=True)
+            probs = e * inv
+            score_s[h] = probs
+            prob_b[:, block(h)] = probs.astype(BF16)
+            inv_end = jnp.where(mine, inv, inv_end)
+        p_end = e_end * inv_end
+        score_s[last] = p_end
+        prob_b[:, block(last)] = p_end.astype(BF16)
+        attended = from_perm(plain(prob_b[...], vexp_s[...])).astype(BF16)
+
+        @pl.when(p + 1 < positions)
+        def _():
+            relay_b(p + 1)
+
+        middle = cells_s[p] + by_t(attended, proj_t[...])
+        normed_two, inv_two = layer_norm(middle)
+        scaled_two = (normed_two * gain_two).astype(BF16)
+        cot = cots_s[p].astype(BF16)
+        activated, slope = gelu_pair(by_t(scaled_two, up_t[...]))
+        g_down[...] += outer(cot, activated.astype(BF16))
+        d_hidden = (plain(cot, down_t[...]) * slope).astype(BF16)
+        g_up[...] += outer(d_hidden, scaled_two)
+        d_htwo = plain(d_hidden, up_t[...])
+        g_gain[1:2] += jnp.sum(d_htwo * normed_two, axis=0, keepdims=True)
+        d_middle = cots_s[p] + norm_back(d_htwo * gain_two, normed_two, inv_two)
+        d_middle_b = d_middle.astype(BF16)
+        g_proj[...] += outer(d_middle_b, attended)
+        dap = to_perm(plain(d_middle_b, proj_t[...])).astype(BF16)
+
+        p_end = score_s[last]
+        dp_end = by_t(dap, vexp_s[block(last)])
+        mix_end = p_end * dp_end
+        dot_end = jnp.zeros((WIN, LANES), F32)
+
+        def put(h, ds):
+            ds_b[:, block(h)] = ds.astype(BF16)
+            for r in range(per):
+                asm_s[pl.ds(r * SUB + h, SUB, stride=WIN), :] = ds[r * SUB : (r + 1) * SUB]
+
+        for h in range(head_count):
+            mine = seg == h
+            probs = score_s[h]
+            dp = by_t(dap, vexp_s[block(h)])
+            dot = jnp.sum(probs * dp + jnp.where(mine, mix_end, 0.0), axis=-1, keepdims=True)
+            dot_end = jnp.where(mine, dot, dot_end)
+            put(h, probs * (dp - dot))
+        put(last, p_end * (dp_end - dot_end))
+        for j in range(owners):
+            t_w[p, j] = asm_s[j * WIN : (j + 1) * WIN].astype(BF16)
+        stage_one(p)
+        d_q = from_perm(plain(ds_b[...], kexp_s[...]))
+        d_k = collapse(outer(ds_b[...], qp))
+        d_v = collapse(outer(prob_b[...], dap))
+        d_hone = jnp.zeros((WIN, features), F32)
+        for i, part in enumerate((d_q * factor, d_k * factor, d_v)):
+            part = part.astype(BF16)
+            span = slice(i * features, (i + 1) * features)
+            g_qkv[span] += outer(part, scaled_one)
+            d_hone = d_hone + plain(part, qkv_t[span])
+        g_gain[0:1] += jnp.sum(d_hone * normed_one, axis=0, keepdims=True)
+        dcell_s[p] = d_middle + norm_back(d_hone * gain_one, normed_one, inv_one)
+
+        @pl.when(p >= 1)
+        def _():
+            stage_two(p - 1)
+
+        @pl.when(p >= 2)
+        def _():
+            stage_three(p - 2)
+
+        @pl.when(p >= 3)
+        def _():
+            stage_four(p - 3)
+
+        return carry
+
+    lax.fori_loop(0, positions, body, 0)
+
+    down = d.shape[1]
+    gain_rows = jnp.concatenate([g_gain[...], jnp.zeros((height - n_up - 2, features), F32)], axis=0)
+    pad = height - n_qkv - n_proj
+    for j in range(owners):
+        ga[0, j] = jnp.concatenate([g_up[j * n_up : (j + 1) * n_up], gain_rows], axis=0).astype(BF16)
+        rows = [g_qkv[j * n_qkv : (j + 1) * n_qkv], g_proj[j * n_proj : (j + 1) * n_proj]]
+        rows += [jnp.zeros((pad, features), F32)] if pad else []
+        ga[1, j] = jnp.concatenate(rows, axis=0).astype(BF16)
+        for i in range(2):
+            gd[i, j] = g_down[j * down : (j + 1) * down, i * wide : (i + 1) * wide].astype(BF16)
+    pairs = [
+        rc(src.at[1 - core], dst, pcs.at[i], pcr.at[i], twin)
+        for i, (src, dst) in enumerate(((ga, a_twin), (gd, d_twin)))
+    ]
+    for copy in pairs:
+        copy.start()
+    for i in range(positions):
+        for j in range(WPL):
+            level = (WPL * i + j + WPL // 2) % levels
+            store_strided(wide_s, level, slab, levels, dcell_s[i, j * slab : (j + 1) * slab])
+    obuf[...] = whole(wide_s).reshape(obuf.shape).astype(BF16)
+    outs = [
+        rc(obuf.at[end_r, first_c], out.at[lo_r, hi_c], ohs.at[0], ohr.at[0], at(1, 0)),
+        rc(obuf.at[first_r, end_c], out.at[hi_r, lo_c], ohs.at[1], ohr.at[1], at(0, 1)),
+        rc(obuf.at[end_r, end_c], out.at[lo_r, lo_c], ohs.at[2], ohr.at[2], at(1, 1)),
+    ]
+    out[hi_r, hi_c] = obuf[first_r, first_c]
+    halves = (a_half, d_half)
+    p_x, p_mid, p_z = (a_x, d_x), (a_mid, d_mid), (a_z, d_z)
+
+    def near_p(i, k):
+        owner = lax.rem(across[1] + 2 * k, nlon)
+        return rc(halves[i].at[owner], p_x[i].at[k], pxs.at[i, k], pxr.at[i, k], across)
+
+    def far_p(i, k):
+        return rc(p_mid[i].at[k], p_z[i].at[k], pzs.at[i, k], pzr.at[i, k], at(0, 2 * k))
+
+    for i, (mine, got) in enumerate(((ga, a_twin), (gd, d_twin))):
+        pairs[i].wait()
+        halves[i][...] = (mine[core].astype(F32) + got[...].astype(F32)).astype(BF16)
+        for k in order:
+            near_p(i, k).start()
+    for copy in outs:
+        copy.start()
+    for p in range(max(positions - 1, 0), positions):
+        stage_two(p)
+    for p in range(max(positions - 2, 0), positions - 1):
+        stage_three(p)
+    for p in range(max(positions - 3, 0), positions - 2):
+        stage_four(p)
+    for i in (0, 1):
+        for k in range(1, reach):
+            owner = lax.rem(lon + 2 * k, nlon)
+            near_p(i, k).wait_recv()
+            p_mid[i][k] = (halves[i][owner].astype(F32) + p_x[i][k].astype(F32)).astype(BF16)
+            far_p(i, k).start()
+    stage_three(positions - 1)
+    for p in range(max(positions - 2, 0), positions - 1):
+        stage_four(p)
+    row = lax.div(lat, 2)
+    lines, fins = (a_row, d_row), (a_fin, d_fin)
+
+    def line_p(i, j):
+        slot = lines[i].at[row]
+        return rc(slot, slot, pls.at[i, j], plr.at[i, j], at(2 * j, 0))
+
+    for i in (0, 1):
+        near_p(i, 0).wait_recv()
+        total = halves[i][lon].astype(F32) + p_x[i][0].astype(F32)
+        for k in range(1, reach):
+            far_p(i, k).wait_recv()
+            total = total + p_z[i][k].astype(F32)
+        lines[i][row] = total.astype(BF16)
+        for j in range(1, rows_n):
+            line_p(i, j).start()
+    stage_four(positions - 1)
+
+    def last_p(i):
+        slot = fins[i].at[core]
+        return rc(slot, slot, pfs.at[i], pfr.at[i], twin)
+
+    for i in (0, 1):
+        for j in range(1, rows_n):
+            line_p(i, j).wait_recv()
+        total = lines[i][0].astype(F32)
+        for j in range(1, rows_n):
+            total = total + lines[i][j].astype(F32)
+        fins[i][core] = total * scale
+        last_p(i).start()
+    for p in range(positions):
+        row_t(p, 0).wait_recv()
+        for j in range(1, rows_n):
+            fold_t(p, j).wait_recv()
+    spots = nlat * positions
+    for i in range(nlat):
+        for p in range(positions):
+            t_val[(i * positions + p) * WIN : (i * positions + p + 1) * WIN] = t_row[i, p].astype(F32)
+    cols_i = lax.broadcasted_iota(jnp.int32, (type_count, spots), 1)
+    want = jnp.full((type_count, spots), -1, jnp.int32)
+    for i in range(nlat):
+        for p in range(positions):
+            want = jnp.where(cols_i == i * positions + p, types[p, i], want)
+    by_type = (lax.broadcasted_iota(jnp.int32, (type_count, spots), 0) == want).astype(F32).astype(BF16)
+    ends = [t_val[pl.ds(r * SUB + head_count, spots, stride=WIN), :] for r in range(per)]
+    for h in range(head_count):
+        pieces = []
+        for r in range(per):
+            pieces.append(t_val[pl.ds(r * SUB + h, spots, stride=WIN), :])
+            pieces.append(ends[r][:, h * spare : (h + 1) * spare])
+        flat = jnp.concatenate(pieces, axis=1).astype(BF16)
+        t_out[h] = jnp.dot(by_type, flat, preferred_element_type=F32)
+    for i in (0, 1):
+        last_p(i).wait_recv()
+    up_o[...] = a_fin[0][:n_up].T
+    qkv_o[...] = a_fin[1][:n_qkv]
+    proj_o[...] = a_fin[1][n_qkv : n_qkv + n_proj]
+    for i in range(2):
+        down_o[:, i * wide : (i + 1) * wide] = d_fin[i]
+    gain_full = a_fin[0][n_up : n_up + 2]
+    count = features // owners
+    mine = gain_full[:, :count]
+    for j in range(1, owners):
+        mine = jnp.where(lon == j, gain_full[:, j * count : (j + 1) * count], mine)
+    gain_o[...] = mine
+    for copy in outs:
+        copy.wait()
+    for i in (0, 1):
+        for k in range(1, reach):
+            far_w(i, k).wait_send()
+            far_p(i, k).wait_send()
+        for k in range(reach):
+            rc(w_slots(lon)[i], w_slots(lon)[i], wxs.at[i, k], wxr.at[i, k], across).wait_send()
+            near_p(i, k).wait_send()
+        for j in range(1, rows_n):
+            line_p(i, j).wait_send()
+        last_p(i).wait_send()
+    for copy in shared:
+        copy.wait_send()
+    for g in (0, 1):
+        for i in range(3):
+            halo(g, i).wait_send()
+    for p in range(positions):
+        for k in range(reach):
+            if k:
+                far_b(p, k).wait_send()
+                far_t(p, k).wait_send()
+            near_b(p, k).wait_send()
+            near_t(p, k).wait_send()
+        for j in range(rows_n):
+            row_t(p, j).wait_send()
+            if j:
+                fold_t(p, j).wait_send()
+
+
+def shards_fused(inputs, cotangent, qkv_weight, proj_weight, up_weight, down_weight, norm_gains, bias_table, type_of, region):
+    levels, rows, cols, features = inputs.shape
+    nlat, nlon = lax.axis_size("lat"), lax.axis_size("lon")
+    level_windows = levels // WPL
+    type_count, head_count, part = bias_table.shape
+    positions, owners, reach, rows_n = level_windows, nlon, nlon // 2, nlat // 2
+    n_up, n_qkv, n_proj = up_weight.shape[1], qkv_weight.shape[1], proj_weight.shape[1]
+    gain_cols, height = norm_gains.shape[1], -(-max(n_up + 2, n_qkv + n_proj) // 8) * 8
+    own_lane = jnp.arange(features, dtype=jnp.int32) // gain_cols == lax.axis_index("lon")
+    gain_rows = jnp.where(own_lane, jnp.tile(norm_gains, (1, nlon)), jnp.zeros((), BF16))
+    gain_rows = jnp.pad(gain_rows, ((0, height - n_up - 2), (0, 0)))
+    a_part = jnp.stack(
+        [
+            jnp.concatenate([up_weight.T, gain_rows]),
+            jnp.pad(
+                jnp.concatenate([qkv_weight.T, proj_weight.T]), ((0, height - n_qkv - n_proj), (0, 0))
+            ),
+        ]
+    )
+    d_part = down_weight.reshape(2, -1, down_weight.shape[1]).transpose(0, 2, 1)
+    labels = region.reshape(level_windows, WPL, rows)
+    labels = jnp.broadcast_to(labels[..., None], labels.shape + (WLON,)).reshape(positions, WIN)
+    label_q = labels.reshape(positions, owners, WIN // owners).transpose(0, 2, 1).reshape(positions, WIN, 1)
+    spare = WIN - LANES
+    ends = jnp.tile(labels[:, LANES:], (1, head_count))
+    ends = jnp.pad(ends, ((0, 0), (0, LANES - head_count * spare)), constant_values=-1)
+    label_k = jnp.stack([labels[:, :LANES], ends], axis=1)
+    dma = pltpu.SemaphoreType.DMA
+    vmem, hbm = pl.BlockSpec(memory_space=pltpu.VMEM), pl.BlockSpec(memory_space=pl.ANY)
+    smem = pl.BlockSpec(memory_space=pltpu.SMEM)
+    cell = (rows, cols, levels, features)
+    blk = (WIN, LANES)
+    wide = (head_count + 1) * LANES
+    down, dw = d_part.shape[1:]
+    a_shape, d_shape = (height, features), (down, dw)
+    sizes = [(owners * n, features) for n in (n_qkv, n_proj, n_up)] + [(features, 2 * dw)]
+    v = pltpu.VMEM
+    scratch = [v((2,) + cell, BF16), v((owners, 2) + a_shape, BF16), v((owners, 2) + d_shape, BF16),
+               v((positions, owners) + blk, BF16)]
+    lane_tiles = -(-features // LANES)
+    scratch += [v((lane_tiles, rows * cols * levels, LANES), F32)] + [v((positions, WIN, features), F32)] * 3
+    scratch += [v((lane_tiles, WIN, LANES), F32), v((owners * WIN, LANES), F32), v((head_count + 1,) + blk, F32)]
+    scratch += [v((WIN, wide), BF16)] * 2 + [v((wide, features), BF16)] * 2
+    scratch += [v((WIN // owners * SUB, LANES), F32)] * 2 + [v((positions, WIN // owners * SUB, LANES), F32)]
+    scratch += [v(size, BF16) for size in sizes] + [v((2, features), F32)]
+    scratch += [v(size, F32) for size in sizes] + [v((2, features), F32)]
+    scratch += [v((2, owners) + a_shape, BF16), v((2, owners) + d_shape, BF16), v(cell, BF16)]
+    scratch += [v((owners,) + s, BF16) for s in (a_shape, d_shape)] * 2
+    scratch += [v((reach,) + s, BF16) for s in (a_shape, d_shape)] * 3
+    scratch += [v((rows_n,) + s, BF16) for s in (a_shape, d_shape)] + [v((2,) + s, F32) for s in (a_shape, d_shape)]
+    scratch += [v((positions, owners) + blk, BF16)] + [v((positions, reach) + blk, BF16)] * 3
+    scratch += [v((nlat, positions) + blk, BF16), v((nlat * positions * WIN, LANES), F32)]
+    scratch += [dma((2,))] + [dma((2, 3))] * 2 + [dma((2, reach))] * 4 + [dma((2, nlon))] * 2
+    scratch += [dma((positions, reach))] * 8 + [dma((positions, rows_n))] * 4
+    scratch += [dma((2,))] * 2 + [dma((2, reach))] * 4 + [dma((2, rows_n))] * 2 + [dma((2,))] * 2 + [dma((3,))] * 2
+    outs = [(cell, BF16), ((n_qkv, features), F32), ((n_proj, features), F32), ((features, n_up), F32),
+            ((down, 2 * dw), F32), ((2, gain_cols), F32), ((head_count, type_count, part), F32)]
+    token_count = levels * rows * cols * nlat * nlon
+    grad, qkv, proj, up, down_g, gain, table = pl.pallas_call(
+        functools.partial(fused_kernel, nlat, nlon, (n_up, n_qkv, n_proj), 1.0 / math.sqrt(token_count)),
+        out_shape=[jax.ShapeDtypeStruct(*o) for o in outs],
+        in_specs=[hbm, hbm, vmem, vmem, vmem, smem, vmem, vmem],
+        out_specs=[vmem] * len(outs),
+        scratch_shapes=scratch,
+        compiler_params=pltpu.CompilerParams(
+            collective_id=0, has_side_effects=True, vmem_limit_bytes=56 * 2**20
+        ),
+    )(
+        inputs.transpose(1, 2, 0, 3), cotangent.transpose(1, 2, 0, 3), a_part, d_part,
+        bias_table.transpose(1, 0, 2), type_of, label_q, label_k,
+    )
+    return grad.transpose(2, 0, 1, 3), qkv.T, proj.T, up, down_g.T, gain, table.transpose(1, 0, 2)
+
+
+def shards(*args):
+    inputs, bias_table = args[0], args[7]
+    nlat, nlon = lax.axis_size("lat"), lax.axis_size("lon")
+    levels, rows, cols, _ = inputs.shape
+    heads = bias_table.shape[1]
+    whole_rows = bias_table.shape[2] * nlon == WIN * WIN and nlon == SUB and WIN % nlon == 0
+    one_window = rows == WLAT and cols == WLON and levels == SUB and nlat % 2 == 0
+    ends_fit = WIN > LANES and (WIN - LANES) * heads <= LANES and heads < SUB
+    tiled = all(args[i].shape[1] % SUB == 0 for i in (2, 3, 4, 5))
+    if whole_rows and one_window and ends_fit and tiled:
+        return shards_fused(*args)
+    return shards_plain(*args)
 
 
 def solution(mesh):

time: 125 us -> 94.1 us (0.75)
  Pallas kernels: 94.2 us -> 76.6 us
  local copies, waits for them, and re-layouts: 28.3 us -> 14.7 us
    pallas_call x4 -> x1, Pallas kernels: 94.2 us -> 76.6 us  [shards_fused(): pl.pallas_call(functools.partial(fused_kernel, nlat, nlon, (n_up, n_qkv,...]
    reshape x20 -> x3, local copies, waits for them, and re-layouts: 8.48 us -> 1.55 us  [the longest x1 0.85 us: shards_fused(): labels.reshape(positions, owners, WIN // owners).transpose(0, 2, 1)]
    unnamed x63 -> x26, local copies, waits for them, and re-layouts: 14.2 us -> 12 us
    another operation x7 -> x5, local copies, waits for them, and re-layouts: 2.34 us -> 0.25 us  [the longest x2 0.09 us: shards_fused(): jnp.tile(norm_gains, (1, nlon))]
    transpose x5 -> x1, local copies, waits for them, and re-layouts: 1.45 us -> 0.1 us  [shards_fused(): labels.reshape(positions, owners, WIN // owners).transpose(0, 2, 1)]
where the time goes in v1:
time: 94.1 us; the launch traced here: 93.3 us
  Pallas kernels  76.6 us (81%)
  local copies, waits for them, and re-layouts  14.7 us (16%)
  other arithmetic  1.31 us (1%)
    pallas_call x1, Pallas kernels, shards_fused(): pl.pallas_call(functools.partial(fused_kernel, nlat, nlon, (n_up, n_qkv,...  76.6 us
    unnamed x26, local copies, waits for them, and re-layouts  12 us

profile of v1, /device:TPU:0, one launch (start us, length us, event | category | flops | bytes accessed | tf_op | source)
XLA Modules:
  0.0 93.3 jit_solution(13826197814787639087)
XLA Ops:
  0.7 0.6 copy-done.8
  1.3 0.1 tile.9
  1.4 0.6 copy-done.6
  2.1 0.1 reshape.34
  2.2 0.1 reshape_reshape.3
  2.3 0.5 copy-done.4
  2.8 0.1 tile.21
  2.9 0.7 slice-done
  3.5 0.6 pad_add_fusion.label_k
  4.1 0.1 copy.21
  4.3 0.6 copy.25
  4.9 0.2 copy-done.1
  5.1 0.1 copy.19
  5.2 0.7 copy-done.2
  5.9 0.7 pad_maximum_fusion.a
  6.6 0.8 reshape.35.label_q
  7.4 76.6 %shard_map.153 = (bf16[6,12,8,192]{3,2,1,0:T(8,128)(2,1)}, f32[72,192]{1,0:T(8,128)}, f32[24,192]{1,0:T(8,128)}, f32[192,96]{1,0:T(8,128)}, f32[24,768]{1,0:T(8,...) custom-call(bf16[6,12,8,192]{3,2,1,0:T(8,128)(2,1)} %bitcast.29, bf16[6,12,8,192]{3,2,1,0:T(8,128)(2,1)} %bitcast.30, ...), custom_call_target="tpu_custom_call" | custom-call | tf_op jit(solution)/shard_map/pallas_call | solution.py:1051
  84.1 1.8 %copy.33 = bf16[8,6,12,192]{3,0,2,1:T(8,128)(2,1)} copy(bf16[8,6,12,192]{3,0,2,1:T(8,128)(2,1)} %bitcast.28) | data formatting | bytes 442368
  85.9 1.5 %copy.34 = f32[192,72]{0,1:T(8,128)} copy(f32[192,72]{0,1:T(8,128)} %bitcast.34) | data formatting | bytes 110592
  87.4 1.3 %copy.35 = f32[192,24]{0,1:T(8,128)} copy(f32[192,24]{0,1:T(8,128)} %bitcast.38) | data formatting | bytes 36864
  88.7 1.5 %copy.36 = f32[192,96]{1,0:T(8,128)} copy(f32[192,96]{1,0:T(8,128)} %get-tuple-element.33) | data formatting | bytes 147456
  90.3 1.5 %copy.37 = f32[768,24]{0,1:T(8,128)} copy(f32[768,24]{0,1:T(8,128)} %bitcast.33) | data formatting | bytes 147456
  91.8 0.6 copy.38
  92.4 1.0 %copy.39 = f32[16,6,2592]{2,0,1:T(8,128)} copy(f32[16,6,2592]{2,0,1:T(8,128)S(1)} %bitcast.26) | data formatting | bytes 1990656
  (22 shorter events, 0.2 us)
Async XLA Ops:
  0.7 0.7 copy-start.8
  1.3 0.7 copy-start.6
  2.2 0.6 copy-start.4
  2.8 0.7 slice-start
  3.5 0.8 copy-start.3
  4.3 0.8 copy-start.1
  5.1 0.8 copy-start.2
  5.1 0.8 copy-start.5
  84.1 8.3 %copy-start = (f32[6,16,2592]{2,1,0:T(8,128)S(1)}, f32[6,16,2592]{2,1,0:T(8,128)}, u32[]{:S(2)}) copy-start(f32[6,16,2592]{2,1,0:T(8,128)} %get-tuple-element.20) | copy-start | bytes 2985988
  90.3 1.5 %copy-start.7 = (f32[2,24]{1,0:T(2,128)S(1)}, f32[2,24]{1,0:T(2,128)}, u32[]{:S(2)}) copy-start(f32[2,24]{1,0:T(2,128)} %get-tuple-element.35) | copy-start | bytes 580

commit v2 on v1

--- a/solution.py
+++ b/solution.py
@@ -468,25 +468,51 @@
     )
 
 
-def fused_kernel(nlat, nlon, cuts, scale, x_in, c_in, a, d, tab, types, label_q, label_k,
+def all_peers(nlat, nlon, at, across):
+    steps = [(0, d) for d in range(2, nlon, 2)] + [(d, 0) for d in range(1, nlat)]
+    steps += [(0, 1), (0, -1), (1, 1), (-1, -1)]
+    return [across] + [at(*step) for step in steps]
+
+
+def finish_kernel(*refs):
+    count = (len(refs) - 1) // 3
+    srcs, dsts, held, sems = refs[:count], refs[count : 2 * count], refs[2 * count : -1], refs[-1]
+    loads = [pltpu.make_async_copy(srcs[i], held[i], sems.at[0, i]) for i in range(count)]
+    stores = [pltpu.make_async_copy(held[i], dsts[i], sems.at[1, i]) for i in range(count)]
+    for copy in loads:
+        copy.start()
+    for load, copy in zip(loads, stores):
+        load.wait()
+        copy.start()
+    for copy in stores:
+        copy.wait()
+
+
+def fused_kernel(nlat, nlon, cuts, scale, x_in, c_in, qkv_in, proj_in, up_in, down_in, gain_in, tab_in, types, region,
                  out, qkv_o, proj_o, up_o, down_o, gain_o, t_out,
+                 qkv_v, proj_v, up_v, down_v, gain_v, tab,
                  grid, a_all, d_all, b_all,
                  wide_s, cells_s, cots_s, dcell_s, perm_s, asm_s, score_s, prob_b, ds_b, kexp_s, vexp_s,
                  pick_m, pick_t, pick_u,
                  qkv_t, proj_t, up_t, down_t, gains, g_qkv, g_proj, g_up, g_down, g_gain,
                  ga, gd, obuf, a_twin, d_twin, a_half, d_half, a_x, d_x, a_mid, d_mid, a_z, d_z, a_row, d_row,
-                 a_fin, d_fin, t_w, t_x, t_mid, t_z, t_row, t_val,
-                 own_s, hs, hr, wzs, wzr, wxs, wxr, wts, wtr, bzs, bzr, bxs, bxr,
-                 txs, txr, tzs, tzr, tls, tlr, tfs, tfr,
-                 pcs, pcr, pxs, pxr, pzs, pzr, pls, plr, pfs, pfr, ohs, ohr):
+                 t_w, t_x, t_mid, t_z, t_row, t_val,
+                 in_s, own_s, hs, hr, wzs, wzr, wxs, wxr, wts, wtr, bzs, bzr, bxs, bxr,
+                 txs, txr, tzs, tzr, tls, tlr,
+                 pcs, pcr, pxs, pxr, pzs, pzr, pls, plr, ohs, ohr):
     n_up, n_qkv, n_proj = cuts
     lat, lon, at, core, twin, across = position(nlat, nlon)
     rows_c, cols_c, levels, features = x_in.shape
     half_r, half_c = rows_c // 2, cols_c // 2
     head_count = tab.shape[0]
     type_count = tab.shape[1]
-    positions = label_q.shape[0]
-    owners, height, wide = nlon, a.shape[1], d.shape[2]
+    positions = types.shape[0]
+    owners, height, wide = nlon, a_all.shape[2], d_all.shape[3]
+    lines_qp, lines_up = (n_qkv + n_proj) // 2, n_up // 2
+    packed_qp, packed_up = lines_qp * 3 // 2, lines_up * 3 // 2
+    side = features - LANES
+    beats = head_count + 1
+    span_b = b_all.shape[2]
     reach, rows_n = nlon // 2, nlat // 2
     head_size = features // head_count
     per = WIN // owners
@@ -494,7 +520,14 @@
     factor = 1.0 / math.sqrt(head_size)
     slab = WIN // WPL
 
-    greet(peers(nlat, nlon, at, twin, across))
+    loads = [
+        pltpu.make_async_copy(src, dst, in_s.at[i])
+        for i, (src, dst) in enumerate(
+            ((qkv_in, qkv_v), (proj_in, proj_v), (up_in, up_v), (gain_in, gain_v), (tab_in, tab), (down_in, down_v))
+        )
+    ]
+    for copy in loads:
+        copy.start()
 
     tiles = [(t, t * LANES, min(LANES, features - t * LANES)) for t in range(-(-features // LANES))]
 
@@ -517,18 +550,17 @@
                 piece = jnp.concatenate([piece, jnp.zeros((size, LANES - count), F32)], axis=1)
             ref.at[t][pl.ds(start, size, stride=stride), :] = piece
 
-    def w_slots(owner):
-        return (a_all.at[owner, core], d_all.at[owner, core])
-
-    w_src = (a.at[core], d.at[core])
-
-    def far_w(i, k):
-        return rc(w_src[i], w_slots(lon)[i], wzs.at[i, k], wzr.at[i, k], at(0, 2 * k))
-
-    for i in (0, 1):
-        for k in range(1, reach):
-            far_w(i, k).start()
-        rc(w_src[i], w_slots(lon)[i], wxs.at[i, 0], wxr.at[i, 0], across).start()
+    def pack(block):
+        half = block.shape[0] // 2
+        return jnp.concatenate(
+            [block[:, :LANES], jnp.concatenate([block[:half, LANES:], block[half:, LANES:]], axis=1)], axis=0
+        )
+
+    def unpack(block):
+        count = block.shape[0] * 2 // 3
+        tail = jnp.concatenate([block[count:, :side], block[count:, side:]], axis=0)
+        return jnp.concatenate([block[:count], tail], axis=1)
+
     lo_r, hi_r = pl.ds(0, half_r), pl.ds(half_r, rows_c - half_r)
     lo_c, hi_c = pl.ds(0, half_c), pl.ds(half_c, cols_c - half_c)
     end_r, end_c = pl.ds(rows_c - half_r, half_r), pl.ds(cols_c - half_c, half_c)
@@ -548,8 +580,66 @@
 
     for g in (0, 1):
         own(g).start()
-        for i in range(3):
-            halo(g, i).start()
+
+    top = packed_qp + SUB
+
+    def w_slot(i, owner):
+        if i == 2:
+            return d_all.at[owner, core]
+        return a_all.at[owner, core].at[pl.ds(0, top) if i == 0 else pl.ds(top, packed_up)]
+
+    def far_w(i, k):
+        return rc(w_slot(i, lon), w_slot(i, lon), wzs.at[i, k], wzr.at[i, k], at(0, 2 * k))
+
+    def near_w(i, k, owner):
+        return rc(w_slot(i, owner), w_slot(i, owner), wxs.at[i, k], wxr.at[i, k], across)
+
+    def pair_w(i, k, owner):
+        return rc(w_slot(i, owner), w_slot(i, owner), wts.at[i, k], wtr.at[i, k], twin)
+
+    def send_w(i):
+        for k in range(1, reach):
+            far_w(i, k).start()
+        near_w(i, 0, lon).start()
+
+    def pass_far(i):
+        for k in range(1, reach):
+            owner = lax.rem(lon - 2 * k + nlon, nlon)
+            far_w(i, k).wait_recv()
+            near_w(i, k, owner).start()
+            pair_w(i, k, owner).start()
+
+    def pass_near(i):
+        for k in range(reach):
+            owner = lax.rem(across[1] - 2 * k + nlon, nlon)
+            near_w(i, k, owner).wait_recv()
+            pair_w(i, reach + k, owner).start()
+
+    def end_pair(i):
+        for k in range(1, 2 * reach):
+            pair_w(i, k, lon).wait_recv()
+
+    greet(all_peers(nlat, nlon, at, across))
+    for i in range(3):
+        halo(0, i).start()
+    for copy in loads[:4]:
+        copy.wait()
+    both = jnp.concatenate([qkv_v[...].astype(F32), proj_v[...].astype(F32)], axis=0)
+    first = up_v[...].astype(F32).T
+    gain_v32 = gain_v[...].astype(F32)
+    gain_rows = jnp.concatenate([gain_v32, jnp.zeros((2, LANES - gain_v32.shape[1]), F32)], axis=1)
+    gain_rows = jnp.concatenate([gain_rows, jnp.zeros((SUB - 2, LANES), F32)], axis=0)
+    for i in range(2):
+        a_all[lon, i] = jnp.concatenate(
+            [
+                pack(both[i * lines_qp : (i + 1) * lines_qp]),
+                gain_rows,
+                pack(first[i * lines_up : (i + 1) * lines_up]),
+            ],
+            axis=0,
+        ).astype(BF16)
+    send_w(0)
+    loads[4].wait()
 
     rows_i = lax.broadcasted_iota(jnp.int32, (SUB, type_count), 0)
     want = jnp.full((SUB, type_count), -1, jnp.int32)
@@ -564,13 +654,12 @@
             end = val[:, r * WIN + LANES : (r + 1) * WIN]
             pick_t[r * SUB : (r + 1) * SUB] = jnp.concatenate([end, jnp.zeros((SUB, LANES - spare), F32)], axis=1)
         for i in range(positions):
-            pick_u[i, pl.ds(h, per, stride=SUB), :] = pick_m[pl.ds(i, per, stride=SUB), :]
+            pick_u[i, pl.ds(h, per, stride=beats), :] = pick_m[pl.ds(i, per, stride=SUB), :]
             piece = pick_t[pl.ds(i, per, stride=SUB), :]
             tails[i] = tails[i] + (pltpu.roll(piece, h * spare, 1) if h else piece)
     for i in range(positions):
-        pick_u[i, pl.ds(head_count, per, stride=SUB), :] = tails[i]
-        for h in range(head_count + 1, SUB):
-            pick_u[i, pl.ds(h, per, stride=SUB), :] = jnp.zeros((per, LANES), F32)
+        pick_u[i, pl.ds(head_count, per, stride=beats), :] = tails[i]
+        pick_u[i, per * beats :, :] = jnp.zeros((span_b - per * beats, LANES), F32)
 
     def far_b(p, k):
         return rc(b_all.at[p, lon], b_all.at[p, lon], bzs.at[p, k], bzr.at[p, k], at(0, 2 * k))
@@ -588,24 +677,23 @@
 
     for i in range(positions):
         b_all[i, lon] = pick_u[i].astype(BF16)
-    for i in range(positions):
+
+    def send_b(p):
         for k in range(1, reach):
-            far_b(i, k).start()
-
-    a_all[lon] = a[...]
-    d_all[lon] = d[...]
-    shared = []
-    for k in range(1, reach):
-        owner = lax.rem(lon - 2 * k + nlon, nlon)
-        for i in (0, 1):
-            slot = w_slots(owner)[i]
-            far_w(i, k).wait_recv()
-            rc(slot, slot, wxs.at[i, k], wxr.at[i, k], across).start()
-            copy = rc(slot, slot, wts.at[i, k], wtr.at[i, k], twin)
-            copy.start()
-            shared.append(copy)
-    relay_b(0)
-    for g, store in ((0, cells_s), (1, cots_s)):
+            far_b(p, k).start()
+
+    send_b(0)
+    loads[5].wait()
+    for i in range(2):
+        d_all[lon, i] = down_v[:, i * wide : (i + 1) * wide]
+    send_w(1)
+    send_w(2)
+    for i in range(3):
+        halo(1, i).start()
+    for i in range(1, positions):
+        send_b(i)
+
+    def windows_of(g, store):
         own(g).wait()
         for i in range(3):
             halo(g, i).wait_recv()
@@ -614,34 +702,39 @@
             for j in range(WPL):
                 level = (WPL * i + j + WPL // 2) % levels
                 store[i, j * slab : (j + 1) * slab] = strided(wide_s, level, slab, levels)
-    for k in range(reach):
-        owner = lax.rem(across[1] - 2 * k + nlon, nlon)
-        for i in (0, 1):
-            slot = w_slots(owner)[i]
-            rc(slot, slot, wxs.at[i, k], wxr.at[i, k], across).wait_recv()
-            copy = rc(slot, slot, wts.at[i, reach + k], wtr.at[i, reach + k], twin)
-            copy.start()
-            shared.append(copy)
+
     for total in (g_qkv, g_proj, g_up, g_down, g_gain):
         total[...] = jnp.zeros(total.shape, F32)
     asm_s[...] = jnp.zeros(asm_s.shape, F32)
-    for copy in shared:
-        copy.wait_recv()
-
-    def joined(half, start, count):
-        rows = [a_all[j, half].astype(F32)[start : start + count] for j in range(owners)]
-        return jnp.concatenate(rows, axis=0).astype(BF16)
-
-    up_t[...] = joined(0, 0, n_up)
-    qkv_t[...] = joined(1, 0, n_qkv)
-    proj_t[...] = joined(1, n_qkv, n_proj)
-    for i in range(2):
-        rows = [d_all[j, i].astype(F32) for j in range(owners)]
-        down_t[:, i * wide : (i + 1) * wide] = jnp.concatenate(rows, axis=0).astype(BF16)
-    gain_sum = a_all[0, 0].astype(F32)[n_up : n_up + 2]
-    for j in range(1, owners):
-        gain_sum = gain_sum + a_all[j, 0].astype(F32)[n_up : n_up + 2]
-    gains[...] = gain_sum
+    pass_far(0)
+    relay_b(0)
+    windows_of(0, cells_s)
+    pass_near(0)
+    pass_far(1)
+    pass_far(2)
+    end_pair(0)
+    for j in range(owners):
+        rows = [unpack(a_all[j, i, :packed_qp].astype(F32)) for i in range(2)]
+        rows = jnp.concatenate(rows, axis=0).astype(BF16)
+        qkv_t[j * n_qkv : (j + 1) * n_qkv] = rows[:n_qkv]
+        proj_t[j * n_proj : (j + 1) * n_proj] = rows[n_qkv:]
+    lanes = features // owners
+    gains[...] = jnp.concatenate(
+        [a_all[j, 0, packed_qp:top].astype(F32)[:2, :lanes] for j in range(owners)], axis=1
+    )
+
+    def late_weights():
+        pass_near(1)
+        pass_near(2)
+        windows_of(1, cots_s)
+        end_pair(1)
+        end_pair(2)
+        for j in range(owners):
+            rows = [unpack(a_all[j, i, top:].astype(F32)) for i in range(2)]
+            up_t[j * n_up : (j + 1) * n_up] = jnp.concatenate(rows, axis=0).astype(BF16)
+        for i in range(2):
+            rows = [d_all[j, i].astype(F32) for j in range(owners)]
+            down_t[:, i * wide : (i + 1) * wide] = jnp.concatenate(rows, axis=0).astype(BF16)
 
     def near_t(p, k):
         owner = lax.rem(across[1] + 2 * k, nlon)
@@ -665,7 +758,7 @@
 
     def row_t(p, j):
         slot = t_row.at[lat, p]
-        return rc(slot, slot, tls.at[p, j], tlr.at[p, j], at(2 * j, 0) if j else twin)
+        return rc(slot, slot, tls.at[p, j], tlr.at[p, j], at(j, 0))
 
     def stage_three(p):
         near_t(p, 0).wait_recv()
@@ -674,17 +767,8 @@
             far_t(p, k).wait_recv()
             total = total + t_z[p, k].astype(F32)
         t_row[lat, p] = total.astype(BF16)
-        for j in list(range(1, rows_n)) + [0]:
+        for j in range(1, nlat):
             row_t(p, j).start()
-
-    def fold_t(p, j):
-        slot = t_row.at[lax.rem(lat - 2 * j + nlat, nlat), p]
-        return rc(slot, slot, tfs.at[p, j], tfr.at[p, j], twin)
-
-    def stage_four(p):
-        for j in range(1, rows_n):
-            row_t(p, j).wait_recv()
-            fold_t(p, j).start()
 
     lane_head = lax.broadcasted_iota(jnp.int32, (1, features), 1) // head_size
     seg = lax.broadcasted_iota(jnp.int32, (1, LANES), 1) // spare
@@ -721,6 +805,19 @@
 
     def block(h):
         return slice(h * LANES, (h + 1) * LANES)
+
+    token_k = lax.broadcasted_iota(jnp.int32, (1, LANES), 1)
+    token_end = LANES + token_k - spare * seg
+    place_q = lax.broadcasted_iota(jnp.int32, (WIN, 1), 0)
+    turn_q = place_q >> (SUB.bit_length() - 1)
+    token_q = per * (place_q - SUB * turn_q) + turn_q
+    cells_r = rows_c * WPL
+
+    def label_of(p, token):
+        label = jnp.full(token.shape, region[WPL * p, 0], jnp.int32)
+        for g in range(1, cells_r):
+            label = jnp.where(token >= cols_c * g, region[WPL * p + g // rows_c, g % rows_c], label)
+        return label
 
     def body(p, carry):
         gain_one, gain_two = gains[0:1], gains[1:2]
@@ -733,12 +830,13 @@
         for j in range(reach):
             near_b(p, j).wait_recv()
         for j in range(owners):
-            asm_s[j * WIN : (j + 1) * WIN] = b_all[p, j].astype(F32)
-        same = label_q[p] == label_k[p, 0:1]
-        same_end = label_q[p] == label_k[p, 1:2]
+            asm_s[j * span_b : (j + 1) * span_b] = b_all[p, j].astype(F32)
+        mine_q = label_of(p, token_q)
+        same = mine_q == label_of(p, token_k)
+        same_end = mine_q == jnp.where(seg < head_count, label_of(p, token_end), -1)
 
         def bias_of(h):
-            return jnp.concatenate([asm_s[pl.ds(r * SUB + h, SUB, stride=WIN), :] for r in range(per)], axis=0)
+            return jnp.concatenate([asm_s[pl.ds(r * beats + h, SUB, stride=span_b), :] for r in range(per)], axis=0)
 
         def raw(h, keep):
             scores = by_t(qp, kexp_s[block(h)]) * factor + bias_of(h)
@@ -768,9 +866,11 @@
         prob_b[:, block(last)] = p_end.astype(BF16)
         attended = from_perm(plain(prob_b[...], vexp_s[...])).astype(BF16)
 
-        @pl.when(p + 1 < positions)
+        @pl.when(p == 0)
         def _():
-            relay_b(p + 1)
+            late_weights()
+            if positions > 1:
+                relay_b(1)
 
         middle = cells_s[p] + by_t(attended, proj_t[...])
         normed_two, inv_two = layer_norm(middle)
@@ -795,7 +895,7 @@
         def put(h, ds):
             ds_b[:, block(h)] = ds.astype(BF16)
             for r in range(per):
-                asm_s[pl.ds(r * SUB + h, SUB, stride=WIN), :] = ds[r * SUB : (r + 1) * SUB]
+                asm_s[pl.ds(r * beats + h, SUB, stride=span_b), :] = ds[r * SUB : (r + 1) * SUB]
 
         for h in range(head_count):
             mine = seg == h
@@ -806,7 +906,7 @@
             put(h, probs * (dp - dot))
         put(last, p_end * (dp_end - dot_end))
         for j in range(owners):
-            t_w[p, j] = asm_s[j * WIN : (j + 1) * WIN].astype(BF16)
+            t_w[p, j] = asm_s[j * span_b : (j + 1) * span_b].astype(BF16)
         stage_one(p)
         d_q = from_perm(plain(ds_b[...], kexp_s[...]))
         d_k = collapse(outer(ds_b[...], qp))
@@ -820,6 +920,10 @@
         g_gain[0:1] += jnp.sum(d_hone * normed_one, axis=0, keepdims=True)
         dcell_s[p] = d_middle + norm_back(d_hone * gain_one, normed_one, inv_one)
 
+        @pl.when(p + 2 < positions)
+        def _():
+            relay_b(p + 2)
+
         @pl.when(p >= 1)
         def _():
             stage_two(p - 1)
@@ -828,23 +932,28 @@
         def _():
             stage_three(p - 2)
 
-        @pl.when(p >= 3)
-        def _():
-            stage_four(p - 3)
-
         return carry
 
     lax.fori_loop(0, positions, body, 0)
 
-    down = d.shape[1]
-    gain_rows = jnp.concatenate([g_gain[...], jnp.zeros((height - n_up - 2, features), F32)], axis=0)
-    pad = height - n_qkv - n_proj
+    down = d_all.shape[2]
+    no_gain = jnp.zeros((SUB, LANES), F32)
     for j in range(owners):
-        ga[0, j] = jnp.concatenate([g_up[j * n_up : (j + 1) * n_up], gain_rows], axis=0).astype(BF16)
-        rows = [g_qkv[j * n_qkv : (j + 1) * n_qkv], g_proj[j * n_proj : (j + 1) * n_proj]]
-        rows += [jnp.zeros((pad, features), F32)] if pad else []
-        ga[1, j] = jnp.concatenate(rows, axis=0).astype(BF16)
+        block_qp = jnp.concatenate(
+            [g_qkv[j * n_qkv : (j + 1) * n_qkv], g_proj[j * n_proj : (j + 1) * n_proj]], axis=0
+        )
+        block_up = g_up[j * n_up : (j + 1) * n_up]
+        own_gain = jnp.concatenate([g_gain[:, j * lanes : (j + 1) * lanes], jnp.zeros((2, LANES - lanes), F32)], axis=1)
+        own_gain = jnp.concatenate([own_gain, jnp.zeros((SUB - 2, LANES), F32)], axis=0)
         for i in range(2):
+            ga[i, j] = jnp.concatenate(
+                [
+                    pack(block_qp[i * lines_qp : (i + 1) * lines_qp]),
+                    no_gain if i else own_gain,
+                    pack(block_up[i * lines_up : (i + 1) * lines_up]),
+                ],
+                axis=0,
+            ).astype(BF16)
             gd[i, j] = g_down[j * down : (j + 1) * down, i * wide : (i + 1) * wide].astype(BF16)
     pairs = [
         rc(src.at[1 - core], dst, pcs.at[i], pcr.at[i], twin)
@@ -884,8 +993,6 @@
         stage_two(p)
     for p in range(max(positions - 2, 0), positions - 1):
         stage_three(p)
-    for p in range(max(positions - 3, 0), positions - 2):
-        stage_four(p)
     for i in (0, 1):
         for k in range(1, reach):
             owner = lax.rem(lon + 2 * k, nlon)
@@ -893,14 +1000,11 @@
             p_mid[i][k] = (halves[i][owner].astype(F32) + p_x[i][k].astype(F32)).astype(BF16)
             far_p(i, k).start()
     stage_three(positions - 1)
-    for p in range(max(positions - 2, 0), positions - 1):
-        stage_four(p)
-    row = lax.div(lat, 2)
-    lines, fins = (a_row, d_row), (a_fin, d_fin)
+    lines = (a_row, d_row)
 
     def line_p(i, j):
-        slot = lines[i].at[row]
-        return rc(slot, slot, pls.at[i, j], plr.at[i, j], at(2 * j, 0))
+        slot = lines[i].at[lat]
+        return rc(slot, slot, pls.at[i, j], plr.at[i, j], at(j, 0))
 
     for i in (0, 1):
         near_p(i, 0).wait_recv()
@@ -908,72 +1012,63 @@
         for k in range(1, reach):
             far_p(i, k).wait_recv()
             total = total + p_z[i][k].astype(F32)
-        lines[i][row] = total.astype(BF16)
-        for j in range(1, rows_n):
+        lines[i][lat] = total.astype(BF16)
+        for j in range(1, nlat):
             line_p(i, j).start()
-    stage_four(positions - 1)
-
-    def last_p(i):
-        slot = fins[i].at[core]
-        return rc(slot, slot, pfs.at[i], pfr.at[i], twin)
-
-    for i in (0, 1):
-        for j in range(1, rows_n):
-            line_p(i, j).wait_recv()
-        total = lines[i][0].astype(F32)
-        for j in range(1, rows_n):
-            total = total + lines[i][j].astype(F32)
-        fins[i][core] = total * scale
-        last_p(i).start()
     for p in range(positions):
-        row_t(p, 0).wait_recv()
-        for j in range(1, rows_n):
-            fold_t(p, j).wait_recv()
+        for j in range(1, nlat):
+            row_t(p, j).wait_recv()
     spots = nlat * positions
     for i in range(nlat):
         for p in range(positions):
-            t_val[(i * positions + p) * WIN : (i * positions + p + 1) * WIN] = t_row[i, p].astype(F32)
+            t_val[(i * positions + p) * span_b : (i * positions + p + 1) * span_b] = t_row[i, p].astype(F32)
     cols_i = lax.broadcasted_iota(jnp.int32, (type_count, spots), 1)
     want = jnp.full((type_count, spots), -1, jnp.int32)
     for i in range(nlat):
         for p in range(positions):
             want = jnp.where(cols_i == i * positions + p, types[p, i], want)
     by_type = (lax.broadcasted_iota(jnp.int32, (type_count, spots), 0) == want).astype(F32).astype(BF16)
-    ends = [t_val[pl.ds(r * SUB + head_count, spots, stride=WIN), :] for r in range(per)]
+    ends = [t_val[pl.ds(r * beats + head_count, spots, stride=span_b), :] for r in range(per)]
     for h in range(head_count):
         pieces = []
         for r in range(per):
-            pieces.append(t_val[pl.ds(r * SUB + h, spots, stride=WIN), :])
+            pieces.append(t_val[pl.ds(r * beats + h, spots, stride=span_b), :])
             pieces.append(ends[r][:, h * spare : (h + 1) * spare])
         flat = jnp.concatenate(pieces, axis=1).astype(BF16)
         t_out[h] = jnp.dot(by_type, flat, preferred_element_type=F32)
+    def total_p(i, half):
+        total = lines[i][half].astype(F32)
+        for j in range(1, rows_n):
+            total = total + lines[i][2 * j + half].astype(F32)
+        return total * scale
+
     for i in (0, 1):
-        last_p(i).wait_recv()
-    up_o[...] = a_fin[0][:n_up].T
-    qkv_o[...] = a_fin[1][:n_qkv]
-    proj_o[...] = a_fin[1][n_qkv : n_qkv + n_proj]
-    for i in range(2):
-        down_o[:, i * wide : (i + 1) * wide] = d_fin[i]
-    gain_full = a_fin[0][n_up : n_up + 2]
-    count = features // owners
-    mine = gain_full[:, :count]
-    for j in range(1, owners):
-        mine = jnp.where(lon == j, gain_full[:, j * count : (j + 1) * count], mine)
-    gain_o[...] = mine
+        for j in range(1, nlat):
+            line_p(i, j).wait_recv()
+    sums = [total_p(0, half) for half in range(2)]
+    up_o[...] = jnp.concatenate([unpack(part[top:]) for part in sums], axis=0).T
+    block_qp = jnp.concatenate([unpack(part[:packed_qp]) for part in sums], axis=0)
+    qkv_o[...] = block_qp[:n_qkv]
+    proj_o[...] = block_qp[n_qkv:]
+    gain_o[...] = sums[0][packed_qp : packed_qp + 2, :lanes]
+    for half in range(2):
+        down_o[:, half * wide : (half + 1) * wide] = total_p(1, half)
     for copy in outs:
         copy.wait()
+    for i in range(3):
+        for k in range(reach):
+            if k:
+                far_w(i, k).wait_send()
+                pair_w(i, k, lon).wait_send()
+            near_w(i, k, lon).wait_send()
+            pair_w(i, reach + k, lon).wait_send()
     for i in (0, 1):
-        for k in range(1, reach):
-            far_w(i, k).wait_send()
-            far_p(i, k).wait_send()
         for k in range(reach):
-            rc(w_slots(lon)[i], w_slots(lon)[i], wxs.at[i, k], wxr.at[i, k], across).wait_send()
+            if k:
+                far_p(i, k).wait_send()
             near_p(i, k).wait_send()
-        for j in range(1, rows_n):
+        for j in range(1, nlat):
             line_p(i, j).wait_send()
-        last_p(i).wait_send()
-    for copy in shared:
-        copy.wait_send()
     for g in (0, 1):
         for i in range(3):
             halo(g, i).wait_send()
@@ -984,10 +1079,8 @@
                 far_t(p, k).wait_send()
             near_b(p, k).wait_send()
             near_t(p, k).wait_send()
-        for j in range(rows_n):
+        for j in range(1, nlat):
             row_t(p, j).wait_send()
-            if j:
-                fold_t(p, j).wait_send()
 
 
 def shards_fused(inputs, cotangent, qkv_weight, proj_weight, up_weight, down_weight, norm_gains, bias_table, type_of, region):
@@ -997,70 +1090,66 @@
     type_count, head_count, part = bias_table.shape
     positions, owners, reach, rows_n = level_windows, nlon, nlon // 2, nlat // 2
     n_up, n_qkv, n_proj = up_weight.shape[1], qkv_weight.shape[1], proj_weight.shape[1]
-    gain_cols, height = norm_gains.shape[1], -(-max(n_up + 2, n_qkv + n_proj) // 8) * 8
-    own_lane = jnp.arange(features, dtype=jnp.int32) // gain_cols == lax.axis_index("lon")
-    gain_rows = jnp.where(own_lane, jnp.tile(norm_gains, (1, nlon)), jnp.zeros((), BF16))
-    gain_rows = jnp.pad(gain_rows, ((0, height - n_up - 2), (0, 0)))
-    a_part = jnp.stack(
-        [
-            jnp.concatenate([up_weight.T, gain_rows]),
-            jnp.pad(
-                jnp.concatenate([qkv_weight.T, proj_weight.T]), ((0, height - n_qkv - n_proj), (0, 0))
-            ),
-        ]
-    )
-    d_part = down_weight.reshape(2, -1, down_weight.shape[1]).transpose(0, 2, 1)
-    labels = region.reshape(level_windows, WPL, rows)
-    labels = jnp.broadcast_to(labels[..., None], labels.shape + (WLON,)).reshape(positions, WIN)
-    label_q = labels.reshape(positions, owners, WIN // owners).transpose(0, 2, 1).reshape(positions, WIN, 1)
-    spare = WIN - LANES
-    ends = jnp.tile(labels[:, LANES:], (1, head_count))
-    ends = jnp.pad(ends, ((0, 0), (0, LANES - head_count * spare)), constant_values=-1)
-    label_k = jnp.stack([labels[:, :LANES], ends], axis=1)
+    gain_cols = norm_gains.shape[1]
+    height = (n_qkv + n_proj + n_up) * 3 // 4 + SUB
+    down, dw = down_weight.shape[1], down_weight.shape[0] // 2
     dma = pltpu.SemaphoreType.DMA
-    vmem, hbm = pl.BlockSpec(memory_space=pltpu.VMEM), pl.BlockSpec(memory_space=pl.ANY)
+    vmem, hbm = pl.BlockSpec(memory_space=pltpu.VMEM), pl.BlockSpec(memory_space=pltpu.HBM)
     smem = pl.BlockSpec(memory_space=pltpu.SMEM)
     cell = (rows, cols, levels, features)
-    blk = (WIN, LANES)
+    per = WIN // owners
+    blk = (-(-per * (head_count + 1) // 16) * 16, LANES)
     wide = (head_count + 1) * LANES
-    down, dw = d_part.shape[1:]
-    a_shape, d_shape = (height, features), (down, dw)
+    a_shape, d_shape = (height, LANES), (down, dw)
     sizes = [(owners * n, features) for n in (n_qkv, n_proj, n_up)] + [(features, 2 * dw)]
     v = pltpu.VMEM
-    scratch = [v((2,) + cell, BF16), v((owners, 2) + a_shape, BF16), v((owners, 2) + d_shape, BF16),
-               v((positions, owners) + blk, BF16)]
     lane_tiles = -(-features // LANES)
+    scratch = [v((n_qkv, features), BF16), v((n_proj, features), BF16), v((features, n_up), BF16)]
+    scratch += [v((down, 2 * dw), BF16), v((2, gain_cols), BF16), v((head_count, type_count, part), BF16)]
+    scratch += [v((2,) + cell, BF16), v((owners, 2) + a_shape, BF16), v((owners, 2) + d_shape, BF16),
+                v((positions, owners) + blk, BF16)]
     scratch += [v((lane_tiles, rows * cols * levels, LANES), F32)] + [v((positions, WIN, features), F32)] * 3
-    scratch += [v((lane_tiles, WIN, LANES), F32), v((owners * WIN, LANES), F32), v((head_count + 1,) + blk, F32)]
+    scratch += [v((lane_tiles, WIN, LANES), F32), v((owners * blk[0], LANES), F32)]
+    scratch += [v((head_count + 1, WIN, LANES), F32)]
     scratch += [v((WIN, wide), BF16)] * 2 + [v((wide, features), BF16)] * 2
-    scratch += [v((WIN // owners * SUB, LANES), F32)] * 2 + [v((positions, WIN // owners * SUB, LANES), F32)]
+    scratch += [v((per * SUB, LANES), F32)] * 2 + [v((positions,) + blk, F32)]
     scratch += [v(size, BF16) for size in sizes] + [v((2, features), F32)]
     scratch += [v(size, F32) for size in sizes] + [v((2, features), F32)]
     scratch += [v((2, owners) + a_shape, BF16), v((2, owners) + d_shape, BF16), v(cell, BF16)]
     scratch += [v((owners,) + s, BF16) for s in (a_shape, d_shape)] * 2
     scratch += [v((reach,) + s, BF16) for s in (a_shape, d_shape)] * 3
-    scratch += [v((rows_n,) + s, BF16) for s in (a_shape, d_shape)] + [v((2,) + s, F32) for s in (a_shape, d_shape)]
+    scratch += [v((nlat,) + s, BF16) for s in (a_shape, d_shape)]
     scratch += [v((positions, owners) + blk, BF16)] + [v((positions, reach) + blk, BF16)] * 3
-    scratch += [v((nlat, positions) + blk, BF16), v((nlat * positions * WIN, LANES), F32)]
-    scratch += [dma((2,))] + [dma((2, 3))] * 2 + [dma((2, reach))] * 4 + [dma((2, nlon))] * 2
-    scratch += [dma((positions, reach))] * 8 + [dma((positions, rows_n))] * 4
-    scratch += [dma((2,))] * 2 + [dma((2, reach))] * 4 + [dma((2, rows_n))] * 2 + [dma((2,))] * 2 + [dma((3,))] * 2
+    scratch += [v((nlat, positions) + blk, BF16), v((nlat * positions * blk[0], LANES), F32)]
+    scratch += [dma((6,)), dma((2,))] + [dma((2, 3))] * 2 + [dma((3, reach))] * 4 + [dma((3, nlon))] * 2
+    scratch += [dma((positions, reach))] * 8 + [dma((positions, nlat))] * 2
+    scratch += [dma((2,))] * 2 + [dma((2, reach))] * 4 + [dma((2, nlat))] * 2 + [dma((3,))] * 2
     outs = [(cell, BF16), ((n_qkv, features), F32), ((n_proj, features), F32), ((features, n_up), F32),
             ((down, 2 * dw), F32), ((2, gain_cols), F32), ((head_count, type_count, part), F32)]
+    outs = [jax.ShapeDtypeStruct(*o) for o in outs]
     token_count = levels * rows * cols * nlat * nlon
-    grad, qkv, proj, up, down_g, gain, table = pl.pallas_call(
+    found = pl.pallas_call(
         functools.partial(fused_kernel, nlat, nlon, (n_up, n_qkv, n_proj), 1.0 / math.sqrt(token_count)),
-        out_shape=[jax.ShapeDtypeStruct(*o) for o in outs],
-        in_specs=[hbm, hbm, vmem, vmem, vmem, smem, vmem, vmem],
+        out_shape=outs,
+        in_specs=[hbm] * 8 + [smem] * 2,
         out_specs=[vmem] * len(outs),
         scratch_shapes=scratch,
         compiler_params=pltpu.CompilerParams(
-            collective_id=0, has_side_effects=True, vmem_limit_bytes=56 * 2**20
+            collective_id=0, has_side_effects=True, vmem_limit_bytes=60 * 2**20
         ),
     )(
-        inputs.transpose(1, 2, 0, 3), cotangent.transpose(1, 2, 0, 3), a_part, d_part,
-        bias_table.transpose(1, 0, 2), type_of, label_q, label_k,
-    )
+        inputs.transpose(1, 2, 0, 3), cotangent.transpose(1, 2, 0, 3),
+        qkv_weight.T, proj_weight.T, up_weight, down_weight.T, norm_gains,
+        bias_table.transpose(1, 0, 2), type_of, region,
+    )
+    grad, qkv, proj, up, down_g, gain, table = pl.pallas_call(
+        finish_kernel,
+        out_shape=outs,
+        in_specs=[hbm] * len(outs),
+        out_specs=[hbm] * len(outs),
+        scratch_shapes=[v(o.shape, o.dtype) for o in outs] + [dma((2, len(outs)))],
+        compiler_params=pltpu.CompilerParams(vmem_limit_bytes=60 * 2**20),
+    )(*found)
     return grad.transpose(2, 0, 1, 3), qkv.T, proj.T, up, down_g.T, gain, table.transpose(1, 0, 2)
 
 
@@ -1072,7 +1161,9 @@
     whole_rows = bias_table.shape[2] * nlon == WIN * WIN and nlon == SUB and WIN % nlon == 0
     one_window = rows == WLAT and cols == WLON and levels == SUB and nlat % 2 == 0
     ends_fit = WIN > LANES and (WIN - LANES) * heads <= LANES and heads < SUB
-    tiled = all(args[i].shape[1] % SUB == 0 for i in (2, 3, 4, 5))
+    n_qkv, n_proj, n_up, down = (args[i].shape[1] for i in (2, 3, 4, 5))
+    tiled = n_qkv % SUB == 0 and (n_qkv + n_proj) % 32 == 0 and n_up % 32 == 0 and down % SUB == 0
+    tiled = tiled and 2 * (inputs.shape[3] - LANES) == LANES
     if whole_rows and one_window and ends_fit and tiled:
         return shards_fused(*args)
     return shards_plain(*args)

time: 94.1 us -> 72.8 us (0.77)
  local copies, waits for them, and re-layouts: 14.7 us -> 0 us
  Pallas kernels: 76.6 us -> 71.9 us
  other arithmetic: 1.31 us -> 0 us
    unnamed x26 -> x0, local copies, waits for them, and re-layouts: 12 us -> none
    pallas_call x1, Pallas kernels: 76.6 us -> 69.4 us  [shards_fused(): pl.pallas_call(functools.partial(fused_kernel, nlat, nlon, (n_up, n_qkv,...]
    pallas_call x0 -> x1, Pallas kernels: none -> 2.54 us  [shards_fused(): pl.pallas_call(finish_kernel, out_shape=outs, in_specs=[hbm] * len(outs),...]
    reshape x3 -> x0, local copies, waits for them, and re-layouts: 1.55 us -> none  [the longest x1 0.85 us: shards_fused(): labels.reshape(positions, owners, WIN // owners).transpose(0, 2, 1)]
    another operation x3 -> x0, other arithmetic: 1.28 us -> none  [the longest x2 0.68 us: shards_fused(): jnp.stack([jnp.concatenate([up_weight.T, gain_rows]), jnp.pad(jnp.concate...]
where the time goes in v2:
time: 72.8 us; the launch traced here: 72.6 us
  Pallas kernels  71.9 us (99%)
    pallas_call x1, Pallas kernels, shards_fused(): pl.pallas_call(functools.partial(fused_kernel, nlat, nlon, (n_up, n_qkv,...  69.4 us
    pallas_call x1, Pallas kernels, shards_fused(): pl.pallas_call(finish_kernel, out_shape=outs, in_specs=[hbm] * len(outs),...  2.54 us

profile of v2, /device:TPU:0, one launch (start us, length us, event | category | flops | bytes accessed | tf_op | source)
XLA Modules:
  0.0 72.6 jit_solution(9749233853054340177)
XLA Ops:
  0.6 69.4 %shard_map.153 = (bf16[6,12,8,192]{3,2,1,0:T(8,128)(2,1)}, f32[72,192]{1,0:T(8,128)}, f32[24,192]{1,0:T(8,128)}, f32[192,96]{1,0:T(8,128)}, f32[24,768]{1,0:T(8,...) custom-call(bf16[6,12,8,192]{3,2,1,0:T(8,128)(2,1)} %bitcast.12, bf16[6,12,8,192]{3,2,1,0:T(8,128)(2,1)} %bitcast.13, ...), custom_call_target="tpu_custom_call" | custom-call | tf_op jit(solution)/shard_map/pallas_call | solution.py:1131
  70.0 2.5 %shard_map.154 = (bf16[6,12,8,192]{3,2,1,0:T(8,128)(2,1)}, f32[72,192]{1,0:T(8,128)}, f32[24,192]{1,0:T(8,128)}, f32[192,96]{1,0:T(8,128)}, f32[24,768]{1,0:T(8,...) custom-call(bf16[6,12,8,192]{3,2,1,0:T(8,128)(2,1)} %get-tuple-element.21.refs_0_, f32[72,192]{1,0:T(8,128)} %get-tuple-element.22.refs_1_, ...), custom_call_target="tpu_custom_call" | custom-call | tf_op jit(solution)/shard_map/pallas_call | solution.py:1145

commit v3 on v2

--- a/solution.py
+++ b/solution.py
@@ -491,7 +491,7 @@
 def fused_kernel(nlat, nlon, cuts, scale, x_in, c_in, qkv_in, proj_in, up_in, down_in, gain_in, tab_in, types, region,
                  out, qkv_o, proj_o, up_o, down_o, gain_o, t_out,
                  qkv_v, proj_v, up_v, down_v, gain_v, tab,
-                 grid, a_all, d_all, b_all,
+                 own_v, tail_v, grid, a_all, d_all, b_all,
                  wide_s, cells_s, cots_s, dcell_s, perm_s, asm_s, score_s, prob_b, ds_b, kexp_s, vexp_s,
                  pick_m, pick_t, pick_u,
                  qkv_t, proj_t, up_t, down_t, gains, g_qkv, g_proj, g_up, g_down, g_gain,
@@ -566,8 +566,10 @@
     end_r, end_c = pl.ds(rows_c - half_r, half_r), pl.ds(cols_c - half_c, half_c)
     first_r, first_c = pl.ds(0, rows_c - half_r), pl.ds(0, cols_c - half_c)
 
+    main = pl.ds(0, LANES)
+
     def halo(g, i):
-        src = (x_in, c_in)[g]
+        src = tail_v if g == 2 else (x_in, c_in)[g].at[:, :, :, main]
         dst = grid.at[g]
         if i == 0:
             return rc(src.at[lo_r, hi_c], dst.at[end_r, first_c], hs.at[g, i], hr.at[g, i], at(-1, 0))
@@ -576,7 +578,7 @@
         return rc(src.at[lo_r, lo_c], dst.at[end_r, end_c], hs.at[g, i], hr.at[g, i], at(-1, -1))
 
     def own(g):
-        return pltpu.make_async_copy((x_in, c_in)[g].at[hi_r, hi_c], grid.at[g].at[first_r, first_c], own_s.at[g])
+        return pltpu.make_async_copy((x_in, c_in)[g], own_v.at[g], own_s.at[g])
 
     for g in (0, 1):
         own(g).start()
@@ -639,6 +641,14 @@
             axis=0,
         ).astype(BF16)
     send_w(0)
+    for g in (0, 1):
+        own(g).wait()
+        grid[g, first_r, first_c] = own_v[g, hi_r, hi_c, :, :LANES]
+    tails = [own_v[g].astype(F32).reshape(-1, features)[:, LANES:] for g in (0, 1)]
+    tail_v[...] = jnp.concatenate(tails, axis=1).reshape(tail_v.shape).astype(BF16)
+    grid[2, first_r, first_c] = tail_v[hi_r, hi_c]
+    for i in range(3):
+        halo(2, i).start()
     loads[4].wait()
 
     rows_i = lax.broadcasted_iota(jnp.int32, (SUB, type_count), 0)
@@ -694,10 +704,13 @@
         send_b(i)
 
     def windows_of(g, store):
-        own(g).wait()
         for i in range(3):
             halo(g, i).wait_recv()
-        fill(wide_s, grid[g].astype(F32).reshape(rows_c * cols_c * levels, features))
+            if g == 0:
+                halo(2, i).wait_recv()
+        wide_s[0] = grid[g].astype(F32).reshape(rows_c * cols_c * levels, LANES)
+        ends = grid[2].astype(F32).reshape(rows_c * cols_c * levels, LANES)
+        wide_s[1, :, :side] = ends[:, g * side : (g + 1) * side]
         for i in range(positions):
             for j in range(WPL):
                 level = (WPL * i + j + WPL // 2) % levels
@@ -1069,7 +1082,7 @@
             near_p(i, k).wait_send()
         for j in range(1, nlat):
             line_p(i, j).wait_send()
-    for g in (0, 1):
+    for g in range(3):
         for i in range(3):
             halo(g, i).wait_send()
     for p in range(positions):
@@ -1106,7 +1119,8 @@
     lane_tiles = -(-features // LANES)
     scratch = [v((n_qkv, features), BF16), v((n_proj, features), BF16), v((features, n_up), BF16)]
     scratch += [v((down, 2 * dw), BF16), v((2, gain_cols), BF16), v((head_count, type_count, part), BF16)]
-    scratch += [v((2,) + cell, BF16), v((owners, 2) + a_shape, BF16), v((owners, 2) + d_shape, BF16),
+    slim = (rows, cols, levels, LANES)
+    scratch += [v((2,) + cell, BF16), v(slim, BF16), v((3,) + slim, BF16), v((owners, 2) + a_shape, BF16), v((owners, 2) + d_shape, BF16),
                 v((positions, owners) + blk, BF16)]
     scratch += [v((lane_tiles, rows * cols * levels, LANES), F32)] + [v((positions, WIN, features), F32)] * 3
     scratch += [v((lane_tiles, WIN, LANES), F32), v((owners * blk[0], LANES), F32)]
@@ -1121,7 +1135,7 @@
     scratch += [v((nlat,) + s, BF16) for s in (a_shape, d_shape)]
     scratch += [v((positions, owners) + blk, BF16)] + [v((positions, reach) + blk, BF16)] * 3
     scratch += [v((nlat, positions) + blk, BF16), v((nlat * positions * blk[0], LANES), F32)]
-    scratch += [dma((6,)), dma((2,))] + [dma((2, 3))] * 2 + [dma((3, reach))] * 4 + [dma((3, nlon))] * 2
+    scratch += [dma((6,)), dma((2,))] + [dma((3, 3))] * 2 + [dma((3, reach))] * 4 + [dma((3, nlon))] * 2
     scratch += [dma((positions, reach))] * 8 + [dma((positions, nlat))] * 2
     scratch += [dma((2,))] * 2 + [dma((2, reach))] * 4 + [dma((2, nlat))] * 2 + [dma((3,))] * 2
     outs = [(cell, BF16), ((n_qkv, features), F32), ((n_proj, features), F32), ((features, n_up), F32),

time: 72.8 us -> 71.2 us (0.978)
  Pallas kernels: 71.9 us -> 70.3 us
    pallas_call x1, Pallas kernels: 69.4 us -> 67.8 us  [shards_fused(): pl.pallas_call(functools.partial(fused_kernel, nlat, nlon, (n_up, n_qkv,...]
where the time goes in v3:
time: 71.2 us; the launch traced here: 71 us
  Pallas kernels  70.3 us (99%)
    pallas_call x1, Pallas kernels, shards_fused(): pl.pallas_call(functools.partial(fused_kernel, nlat, nlon, (n_up, n_qkv,...  67.8 us
    pallas_call x1, Pallas kernels, shards_fused(): pl.pallas_call(finish_kernel, out_shape=outs, in_specs=[hbm] * len(outs),...  2.54 us

profile of v3, /device:TPU:0, one launch (start us, length us, event | category | flops | bytes accessed | tf_op | source)
XLA Modules:
  0.0 71.0 jit_solution(4507678432209170758)
XLA Ops:
  0.6 67.8 %shard_map.153 = (bf16[6,12,8,192]{3,2,1,0:T(8,128)(2,1)}, f32[72,192]{1,0:T(8,128)}, f32[24,192]{1,0:T(8,128)}, f32[192,96]{1,0:T(8,128)}, f32[24,768]{1,0:T(8,...) custom-call(bf16[6,12,8,192]{3,2,1,0:T(8,128)(2,1)} %bitcast.12, bf16[6,12,8,192]{3,2,1,0:T(8,128)(2,1)} %bitcast.13, ...), custom_call_target="tpu_custom_call" | custom-call | tf_op jit(solution)/shard_map/pallas_call | solution.py:1145
  68.4 2.5 %shard_map.154 = (bf16[6,12,8,192]{3,2,1,0:T(8,128)(2,1)}, f32[72,192]{1,0:T(8,128)}, f32[24,192]{1,0:T(8,128)}, f32[192,96]{1,0:T(8,128)}, f32[24,768]{1,0:T(8,...) custom-call(bf16[6,12,8,192]{3,2,1,0:T(8,128)(2,1)} %get-tuple-element.21.refs_0_, f32[72,192]{1,0:T(8,128)} %get-tuple-element.22.refs_1_, ...), custom_call_target="tpu_custom_call" | custom-call | tf_op jit(solution)/shard_map/pallas_call | solution.py:1159
